TPU v7x, 128 devices: a whole 4x4x4 slice. The times are simulated.
128 devices in a mesh: ctx: 32 (over z, y, core), head: 4 (over x).
Axes of the slice: x: 4, y: 4, z: 4, core: 2. Of those that a mesh axis runs over, the one named last changes fastest.
Arguments:
- queries: bfloat16 [49152, 2048], P('ctx', 'head'), may hold values from -20 to 20
- keys: bfloat16 [49152, 2048], P('ctx', 'head'), may hold values from -20 to 20
- values: bfloat16 [49152, 2048], P('ctx', 'head'), may hold values from -6 to 6
- offsets: int32 [3, 16], replicated, may hold values from 0 to 7, as said below
- out_weight: bfloat16 [2048, 2048], replicated, may hold values from -1.1953125 to 1.1953125
Outputs:
- mixed: bfloat16 [49152, 2048], P(('ctx', 'head'))
Inputs may be any that keep to these rules, and one draw needn't show every extreme that they name: `offsets`: each offset of row k - 1 lies in 0 to 2^k - 1; in the last row every value of that range occurs.
All inputs are finite; a program needn't handle non-finite values.
Results may differ from a plain program's by a relative error of at most 0.0053.
Values may be sent and summed in bfloat16 or wider, within the bound.
A program may use at most 192 MiB of HBM per device.

v0:
```python
import math

import jax
import jax.numpy as jnp
from jax import lax
from jax.sharding import PartitionSpec as P

DH = 128
LEVELS = 4


NEG_FILL = -1e30


def swapped(value, axis, bit):
    mask = 2**bit
    pairs = [(source, source ^ mask) for source in range(lax.axis_size(axis))]
    return lax.ppermute(value, axis, pairs)


def pick_rows(source, shifts, dilation):
    hits = jnp.arange(dilation)[:, None] == shifts[None, :]
    shaped = source.reshape(source.shape[0] // dilation, dilation, source.shape[1], source.shape[2])
    return jnp.sum(jnp.where(hits[None, :, :, None], shaped, jnp.zeros((), source.dtype)), axis=1)


def block_attend(query_rows, key_rows, value_rows, query_pos):
    number = query_rows.shape[0]
    heads_here = query_rows.shape[1]
    width_head = query_rows.shape[2]
    height = 512 if number % 512 == 0 else number
    blocks = number // height
    key_pos = jnp.arange(key_rows.shape[0])
    factor = 1.0 / math.sqrt(width_head)

    def one_block(items):
        rows_now, pos_now = items
        scores = (
            jnp.einsum("qhd,khd->hqk", rows_now, key_rows, preferred_element_type=jnp.float32)
            * factor
        )
        scores = jnp.where(pos_now[None, :, None] >= key_pos[None, None, :], scores, NEG_FILL)
        row_max = jnp.max(scores, axis=2)
        weights = jnp.exp(scores - row_max[:, :, None])
        row_sum = jnp.sum(weights, axis=2)
        weighted = jnp.einsum(
            "hqk,khd->qhd",
            weights.astype(jnp.bfloat16),
            value_rows,
            preferred_element_type=jnp.float32,
        )
        return (row_max.T, row_sum.T, weighted)

    shaped_rows = query_rows.reshape(blocks, height, heads_here, width_head)
    maxima, sums_all, outputs = lax.map(one_block, (shaped_rows, query_pos.reshape(blocks, height)))
    return (
        maxima.reshape(number, heads_here),
        sums_all.reshape(number, heads_here),
        outputs.reshape(number, heads_here, width_head),
    )


def spread_rows(parts, shifts, dilation):
    row_max, row_sum, weighted = parts
    hits = jnp.arange(dilation)[:, None] == shifts[None, :]
    number = row_max.shape[0] * dilation
    heads_here = row_max.shape[1]
    full_max = jnp.where(hits[None], row_max[:, None, :], NEG_FILL).reshape(number, heads_here)
    full_sum = jnp.where(hits[None], row_sum[:, None, :], 0.0).reshape(number, heads_here)
    full_out = jnp.where(hits[None, :, :, None], weighted[:, None], 0.0).reshape(
        number, heads_here, weighted.shape[2]
    )
    return (full_max, full_sum, full_out)


def merge_levels(running, fresh):
    new_max = jnp.maximum(running[0], fresh[0])
    old_scale = jnp.exp(running[0] - new_max)
    new_scale = jnp.exp(fresh[0] - new_max)
    new_sum = running[1] * old_scale + fresh[1] * new_scale
    new_out = running[2] * old_scale[:, :, None] + fresh[2] * new_scale[:, :, None]
    return (new_max, new_sum, new_out)


def join_pair(mine, partner, ctx_index, bit_index):
    upper = ctx_index // 2**bit_index % 2 == 1
    joined = []
    for mine_part, other_part in zip(mine, partner):
        joined.append(
            jnp.where(
                upper,
                jnp.concatenate([other_part, mine_part], 0),
                jnp.concatenate([mine_part, other_part], 0),
            )
        )
    return tuple(joined)


def body(queries, keys, values, offsets, out_weight):
    rows_here = queries.shape[0]
    head_count = lax.axis_size("head")
    heads_here = offsets.shape[1] // head_count
    query_heads = queries.reshape(rows_here, heads_here, DH)
    key_heads = keys.reshape(rows_here, heads_here, DH)
    value_heads = values.reshape(rows_here, heads_here, DH)
    ctx_index = lax.axis_index("ctx")
    shifts_here = lax.dynamic_slice_in_dim(
        offsets, lax.axis_index("head") * heads_here, heads_here, 1
    )
    running = block_attend(query_heads, key_heads, value_heads, jnp.arange(rows_here))
    group = (key_heads, value_heads)
    sources = []
    for bit_index in range(LEVELS - 1):
        partner = swapped((group[0], group[1]), "ctx", bit_index)
        group = join_pair(group, partner, ctx_index, bit_index)
        dilation = 2 ** (bit_index + 1)
        sources.append(
            (
                pick_rows(group[0], shifts_here[bit_index], dilation),
                pick_rows(group[1], shifts_here[bit_index], dilation),
            )
        )
    for level_index in range(1, LEVELS):
        dilation = 2**level_index
        shifts_now = shifts_here[level_index - 1]
        query_rows = pick_rows(query_heads, shifts_now, dilation)
        span = rows_here // dilation
        query_pos = ctx_index % dilation * span + jnp.arange(span)
        parts = block_attend(
            query_rows, sources[level_index - 1][0], sources[level_index - 1][1], query_pos
        )
        running = merge_levels(running, spread_rows(parts, shifts_now, dilation))
    attended = (
        (running[2] / running[1][:, :, None])
        .astype(jnp.bfloat16)
        .reshape(rows_here, heads_here * DH)
    )
    regrouped = lax.all_to_all(attended, "head", split_axis=0, concat_axis=1, tiled=True)
    mixed = jnp.dot(regrouped, out_weight, preferred_element_type=jnp.float32)
    return mixed.astype(jnp.bfloat16)


def solution(mesh):
    placed = (P("ctx", "head"), P("ctx", "head"), P("ctx", "head"), P(), P())
    return jax.shard_map(
        body, mesh=mesh, in_specs=placed, out_specs=P(("ctx", "head"), None), check_vma=False
    )
```

profile of v0, /device:TPU:0, one launch (start us, length us, event | category | flops | bytes accessed | tf_op | source)
XLA Modules:
  0.0 672.1 jit_solution(2948327554374246019)
XLA Ops:
  22.7 45.2 %while.3 = (s32[]{:T(128)}, f32[3,512,4]{1,2,0:T(4,128)S(1)}, f32[3,512,4]{1,2,0:T(4,128)}, f32[3,512,4,128]{3,2,1,0:T(4,128)}, s32[3,512]{1,0:T(4,128)S(1)}, /*...) while((s32[]{:T(128)}, f32[3,512,4]{1,2,0:T(4,128)S(1)}, ...), condition=%wide.region_3.4_spmd.clone, body=%wide.region_0.3_spmd.clone.sunk | while | flops 1645998080 | bytes 48830580 | solution.py:55
  91.7 5.8 broadcast_in_dim.426
  100.7 6.7 broadcast_in_dim.441
  137.6 42.4 %fusion.32 = (bf16[1536,4,128]{2,0,1:T(8,128)(2,1)S(1)}, bf16[1536,4,128]{2,0,1:T(8,128)(2,1)S(1)}) fusion(bf16[1536,2,4,128]{3,1,0,2:T(2,128)(2,1)} %bitcast.100, pred[2,4]{0,1:T(4,128)(4,1)S(1)} %copy-done.28, bf16[1536,2,4,128]{3,1,0,2:T(2,128)(2,1)} %bitcast.101), kind=kLoop, calls=%fused_computation.52 | loop fusion | flops 4718592 | bytes 9437192 | tf_op jit(solution)/shard_map/reduce_sum | solution.py:24
  180.1 8.7 %fusion.14 = (f32[4,768]{1,0:T(4,128)S(1)}, f32[4,768,1536]{2,1,0:T(8,128)}) fusion(pred[768,1536]{1,0:T(8,128)(4,1)S(1)} %copy-done.5, bf16[1536,4,128]{2,0,1:T(8,128)(2,1)S(1)} %get-tuple-element.181, bf16[768,4,128]{2,1,0:T(4,128)(2,1)S(1)} %copy-done.10), kind=kOutput, calls=%fused_computation.21 | convolution fusion | flops 1222112256 | bytes 22425600 | tf_op jit(solution)/shard_map/while/body/eval_jaxpr/qhd,khd->hqk/dot_general | solution.py:39
  188.7 7.1 %maximum_select_fusion.3 = bf16[6144,4,128]{0,2,1:T(8,128)(2,1)} fusion(bf16[3072,4,128]{0,2,1:T(8,128)(2,1)S(1)} %maximum_select_fusion.5, bf16[3072,4,128]{0,2,1:T(8,128)(2,1)} %collective-permute-done.3, pred[]{:T(512)S(6)} %eq.62), kind=kLoop, calls=%fused_computation.38 | loop fusion | flops 28311552 | bytes 12582913 | tf_op jit(solution)/shard_map/jit(_where)/select_n | solution.py:90
  199.1 10.6 %fusion.40 = f32[768,4,128]{0,2,1:T(8,128)} fusion(bf16[1536,4,128]{2,0,1:T(8,128)(2,1)S(1)} %get-tuple-element.180, f32[4,768,1536]{2,1,0:T(8,128)} %get-tuple-element.221, f32[4,768]{1,0:T(4,128)S(1)} %get-tuple-element.220, pred[768,1536]{1,0:T(8,128)(4,1)S(1)} %copy-done.5), kind=kOutput, calls=%fused_computation.67 | convolution fusion | flops 1226833920 | bytes 23212032 | tf_op jit(solution)/shard_map/while/body/eval_jaxpr/hqk,khd->qhd/dot_general | solution.py:46
  213.4 10.6 %collective-permute-done.2 = bf16[3072,4,128]{0,2,1:T(8,128)(2,1)} collective-permute-done((bf16[3072,4,128]{0,2,1:T(8,128)(2,1)}, bf16[3072,4,128]{0,2,1:T(8,128)(2,1)}, u32[]{:S(2)}, u32[]{:S(2)}) %collective-permute-start.2) | collective-permute-done | bytes 3145760 | tf_op jit(solution)/shard_map/ppermute | solution.py:18
  224.0 7.1 %maximum_select_fusion.2 = bf16[6144,4,128]{0,2,1:T(8,128)(2,1)} fusion(bf16[3072,4,128]{0,2,1:T(8,128)(2,1)S(1)} %copy-done.3, bf16[3072,4,128]{0,2,1:T(8,128)(2,1)} %collective-permute-done.2, pred[]{:T(512)S(6)} %eq.62), kind=kLoop, calls=%fused_computation.37 | loop fusion | flops 28311552 | bytes 12582913 | tf_op jit(solution)/shard_map/jit(_where)/select_n | solution.py:90
  234.4 9.2 %fusion.15 = f32[4,768]{1,0:T(4,128)S(1)} fusion(f32[4,768,1536]{2,1,0:T(8,128)} %get-tuple-element.221, f32[4,768]{1,0:T(4,128)S(1)} %get-tuple-element.220, pred[768,1536]{1,0:T(8,128)(4,1)S(1)} %copy-done.6), kind=kLoop, calls=%fused_computation.22 | loop fusion | flops 18871296 | bytes 20078592 | tf_op jit(solution)/shard_map/while/body/eval_jaxpr/reduce_sum | solution.py:45
  250.7 8.7 %copy.92 = bf16[6144,4,128]{2,0,1:T(8,128)(2,1)} copy(bf16[6144,4,128]{0,2,1:T(8,128)(2,1)} %maximum_select_fusion.3) | data formatting | bytes 12582912 | tf_op jit(solution)/shard_map/jit(_where)/select_n | solution.py:90
  259.4 8.6 %copy.88 = bf16[6144,4,128]{2,0,1:T(8,128)(2,1)} copy(bf16[6144,4,128]{0,2,1:T(8,128)(2,1)} %maximum_select_fusion.2) | data formatting | bytes 12582912 | tf_op jit(solution)/shard_map/jit(_where)/select_n | solution.py:90
  268.0 42.8 %select_reduce_fusion = (bf16[1536,4,128]{2,0,1:T(8,128)(2,1)S(1)}, bf16[1536,4,128]{2,0,1:T(8,128)(2,1)S(1)}) fusion(bf16[1536,4,4,128]{3,1,0,2:T(4,128)(2,1)} %bitcast.97, pred[4,4]{0,1:T(4,128)(4,1)S(1)} %copy-done.26, bf16[1536,4,4,128]{3,1,0,2:T(4,128)(2,1)} %bitcast.98), kind=kLoop, calls=%fused_computation.39 | loop fusion | flops 11010048 | bytes 15728656 | tf_op jit(solution)/shard_map/reduce_sum | solution.py:24
  324.2 6.4 fusion.23
  336.3 25.0 %collective-permute-done.5 = bf16[6144,4,128]{0,2,1:T(8,128)(2,1)} collective-permute-done((bf16[6144,4,128]{0,2,1:T(8,128)(2,1)}, bf16[6144,4,128]{0,2,1:T(8,128)(2,1)}, u32[]{:S(2)}, u32[]{:S(2)}) %collective-permute-start.5) | collective-permute-done | bytes 6291488 | tf_op jit(solution)/shard_map/ppermute | solution.py:18
  361.4 15.6 %maximum_select_fusion.1 = bf16[12288,4,128]{0,2,1:T(8,128)(2,1)} fusion(bf16[6144,4,128]{0,2,1:T(8,128)(2,1)} %maximum_select_fusion.3, bf16[6144,4,128]{0,2,1:T(8,128)(2,1)} %collective-permute-done.5, pred[]{:T(512)S(6)} %eq.66), kind=kLoop, calls=%fused_computation.25 | loop fusion | flops 56623104 | bytes 25165824 | tf_op jit(solution)/shard_map/jit(_where)/select_n | solution.py:90
  377.0 16.6 %copy.100 = bf16[12288,4,128]{2,0,1:T(8,128)(2,1)} copy(bf16[12288,4,128]{0,2,1:T(8,128)(2,1)} %maximum_select_fusion.1) | data formatting | bytes 25165824 | tf_op jit(solution)/shard_map/jit(_where)/select_n | solution.py:90
  393.6 101.6 %collective-permute-done.4 = bf16[6144,4,128]{0,2,1:T(8,128)(2,1)} collective-permute-done((bf16[6144,4,128]{0,2,1:T(8,128)(2,1)}, bf16[6144,4,128]{0,2,1:T(8,128)(2,1)}, u32[]{:S(2)}, u32[]{:S(2)}) %collective-permute-start.4) | collective-permute-done | bytes 6291488 | tf_op jit(solution)/shard_map/ppermute | solution.py:18
  495.3 15.5 %maximum_select_fusion = bf16[12288,4,128]{0,2,1:T(8,128)(2,1)} fusion(bf16[6144,4,128]{0,2,1:T(8,128)(2,1)} %maximum_select_fusion.2, bf16[6144,4,128]{0,2,1:T(8,128)(2,1)} %collective-permute-done.4, pred[]{:T(512)S(6)} %eq.66), kind=kLoop, calls=%fused_computation.24 | loop fusion | flops 56623104 | bytes 25165824 | tf_op jit(solution)/shard_map/jit(_where)/select_n | solution.py:90
  510.8 16.6 %copy.96 = bf16[12288,4,128]{2,0,1:T(8,128)(2,1)} copy(bf16[12288,4,128]{0,2,1:T(8,128)(2,1)} %maximum_select_fusion) | data formatting | bytes 25165824 | tf_op jit(solution)/shard_map/jit(_where)/select_n | solution.py:90
  527.3 38.2 %fusion.17 = (bf16[1536,4,128]{2,0,1:T(8,128)(2,1)S(1)}, bf16[1536,4,128]{2,0,1:T(8,128)(2,1)S(1)}) fusion(bf16[12288,4,128]{2,0,1:T(8,128)(2,1)} %copy.100, pred[8,4]{0,1:T(4,128)(4,1)S(1)} %iota_compare_fusion.4, bf16[12288,4,128]{2,0,1:T(8,128)(2,1)} %copy.96), kind=kLoop, calls=%fused_computation.27 | loop fusion | flops 23592960 | bytes 28311584 | tf_op jit(solution)/shard_map/reduce_sum | solution.py:24
  627.8 10.9 %divide_convert_fusion = bf16[4,384,512]{2,1,0:T(8,128)(2,1)S(1)} fusion(f32[4,384,512]{2,1,0:T(8,128)} %div.35, f32[4,384,512]{2,1,0:T(8,128)} %mul.164, pred[4,384,512]{2,1,0:T(8,128)(4,1)} %broadcast_in_dim.456, f32[4,384,512]{2,1,0:T(8,128)S(1)} %bitcast.99, f32[4,384,512]{2,1,0:T(8,128)} %mul.161, f32[4,384,512]{2,1,0:T(8,128)} %mul.156, ...), kind=kLoop, calls=%fused_computation.55 | loop fusion | flops 11010048 | bytes 38535168 | tf_op jit(solution)/shard_map/convert_element_type | solution.py:135
  638.8 24.1 %all_to_all.16 = bf16[4,384,512]{2,1,0:T(8,128)(2,1)S(1)} all-to-all(bf16[4,384,512]{2,1,0:T(8,128)(2,1)S(1)} %divide_convert_fusion), channel_id=1, replica_groups=mesh['ctx'=32,'head'=4] {'head'}, dimensions={0} | all-to-all | bytes 3145728 | tf_op jit(solution)/shard_map/all_to_all | solution.py:138
  663.8 8.1 %convolution_convert_fusion = bf16[384,2048]{1,0:T(8,128)(2,1)} fusion(bf16[384,2048]{0,1:T(8,128)(2,1)S(1)} %bitcast.105, bf16[2048,2048]{1,0:T(8,128)(2,1)} %param.11), kind=kOutput, calls=%fused_computation.56 | convolution fusion | flops 3222011904 | bytes 11534336 | tf_op jit(solution)/shard_map/dot_general | solution.py:139
  (188 shorter events, 224.1 us)
Async XLA Ops:
  0.0 20.9 %copy-start = (s32[3,16]{1,0:T(4,128)S(1)}, s32[3,16]{1,0:T(4,128)}, u32[]{:S(2)}) copy-start(s32[3,16]{1,0:T(4,128)} %param.10) | copy-start | bytes 580
  2.6 78.9 %collective-permute-start.1 = (bf16[1536,4,128]{0,2,1:T(8,128)(2,1)}, bf16[1536,4,128]{0,2,1:T(8,128)(2,1)}, u32[]{:S(2)}, u32[]{:S(2)}) collective-permute-start(bf16[1536,4,128]{0,2,1:T(8,128)(2,1)} %bitcast.1), channel_id=1, source_target_pairs={{0,4},{4,0},{8,12},{12,8},{16,20},{20,16},{24,28},{28,24},{32,36},... | collective-permute-start | bytes 4718600 | tf_op jit(solution)/shard_map/ppermute | solution.py:18
  5.2 122.3 %collective-permute-start = (bf16[1536,4,128]{0,2,1:T(8,128)(2,1)}, bf16[1536,4,128]{0,2,1:T(8,128)(2,1)}, u32[]{:S(2)}, u32[]{:S(2)}) collective-permute-start(bf16[1536,4,128]{0,2,1:T(8,128)(2,1)} %bitcast), channel_id=1, source_target_pairs={{0,4},{4,0},{8,12},{12,8},{16,20},{20,16},{24,28},{28,24},{32,36},... | collective-permute-start | bytes 4718600 | tf_op jit(solution)/shard_map/ppermute | solution.py:18
  21.2 65.9 %copy-start.25 = (pred[4,4]{0,1:T(4,128)(4,1)}, pred[4,4]{0,1:T(4,128)(4,1)S(1)}, u32[]{:S(2)}) copy-start(pred[4,4]{0,1:T(4,128)(4,1)S(1)} %iota_compare_fusion.5) | copy-start | bytes 52
  68.0 17.5 %copy-start.23 = (f32[3,512,4]{1,2,0:T(4,128)}, f32[3,512,4]{1,2,0:T(4,128)S(1)}, u32[]{:S(2)}) copy-start(f32[3,512,4]{1,2,0:T(4,128)S(1)} %get-tuple-element.116) | copy-start | bytes 73732
  68.0 9.8 %copy-start.4 = (bf16[1536,512]{1,0:T(8,128)(2,1)S(1)}, bf16[1536,512]{1,0:T(8,128)(2,1)}, u32[]{:S(2)}) copy-start(bf16[1536,512]{1,0:T(8,128)(2,1)} %param.7) | copy-start | bytes 4718596
  77.8 10.9 %copy-start.28 = (pred[2,4]{0,1:T(4,128)(4,1)S(1)}, pred[2,4]{0,1:T(4,128)(4,1)}, u32[]{:S(2)}) copy-start(pred[2,4]{0,1:T(4,128)(4,1)} %copy-done.27) | copy-start | bytes 28
  85.4 103.3 %collective-permute-start.3 = (bf16[3072,4,128]{0,2,1:T(8,128)(2,1)S(1)}, bf16[3072,4,128]{0,2,1:T(8,128)(2,1)}, u32[]{:S(2)}, u32[]{:S(2)}) collective-permute-start(bf16[3072,4,128]{0,2,1:T(8,128)(2,1)S(1)} %maximum_select_fusion.5), channel_id=1, source_target_pairs={{0,8},{4,12},{8,0},{12,4},{16,24},{20,28},{24,16},{28,20},{32,40},... | collective-permute-start | bytes 9437192 | tf_op jit(solution)/shard_map/ppermute | solution.py:18
  90.6 19.9 %copy-start.14 = (pred[1536,4]{1,0:T(8,128)(4,1)S(1)}, pred[1536,4]{1,0:T(8,128)(4,1)}, u32[]{:S(2)}) copy-start(pred[1536,4]{1,0:T(8,128)(4,1)} %copy.99) | copy-start | bytes 18436
  110.5 14.0 %copy-start.29 = (s32[192]{0:T(256)S(1)}, s32[192]{0:T(256)}, u32[]{:S(2)}) copy-start(s32[192]{0:T(256)} %iota_add_fusion.2) | copy-start | bytes 2308
  137.2 86.8 %collective-permute-start.2 = (bf16[3072,4,128]{0,2,1:T(8,128)(2,1)}, bf16[3072,4,128]{0,2,1:T(8,128)(2,1)}, u32[]{:S(2)}, u32[]{:S(2)}) collective-permute-start(bf16[3072,4,128]{0,2,1:T(8,128)(2,1)} %maximum_select_fusion.4), channel_id=1, source_target_pairs={{0,8},{4,12},{8,0},{12,4},{16,24},{20,28},{24,16},{28,20},{32,40},... | collective-permute-start | bytes 9437192 | tf_op jit(solution)/shard_map/ppermute | solution.py:18
  137.6 42.4 %copy-start.5 = (pred[768,1536]{1,0:T(8,128)(4,1)S(1)}, pred[768,1536]{1,0:T(8,128)(4,1)}, u32[]{:S(2)}) copy-start(pred[768,1536]{1,0:T(8,128)(4,1)} %iota_compare_fusion.1) | copy-start | bytes 3538948
  137.6 42.5 %copy-start.10 = (bf16[768,4,128]{2,1,0:T(4,128)(2,1)S(1)}, bf16[768,4,128]{2,1,0:T(4,128)(2,1)}, u32[]{:S(2)}) copy-start(bf16[768,4,128]{2,1,0:T(4,128)(2,1)} %select_reduce_fusion.3) | copy-start | bytes 2359300
  195.8 165.6 %collective-permute-start.5 = (bf16[6144,4,128]{0,2,1:T(8,128)(2,1)}, bf16[6144,4,128]{0,2,1:T(8,128)(2,1)}, u32[]{:S(2)}, u32[]{:S(2)}) collective-permute-start(bf16[6144,4,128]{0,2,1:T(8,128)(2,1)} %maximum_select_fusion.3), channel_id=1, source_target_pairs={{0,16},{4,20},{8,24},{12,28},{16,0},{20,4},{24,8},{28,12},{32,48},... | collective-permute-start | bytes 18874376 | tf_op jit(solution)/shard_map/ppermute | solution.py:18
  209.7 14.2 %copy-start.3 = (bf16[3072,4,128]{0,2,1:T(8,128)(2,1)S(1)}, bf16[3072,4,128]{0,2,1:T(8,128)(2,1)}, u32[]{:S(2)}) copy-start(bf16[3072,4,128]{0,2,1:T(8,128)(2,1)} %maximum_select_fusion.4) | copy-start | bytes 9437188
  213.4 21.0 %copy-start.6 = (pred[768,1536]{1,0:T(8,128)(4,1)S(1)}, pred[768,1536]{1,0:T(8,128)(4,1)}, u32[]{:S(2)}) copy-start(pred[768,1536]{1,0:T(8,128)(4,1)} %iota_compare_fusion.1) | copy-start | bytes 3538948
  231.1 13.9 %copy-start.12 = (f32[768,4]{1,0:T(8,128)S(1)}, f32[768,4]{1,0:T(8,128)}, u32[]{:S(2)}) copy-start(f32[768,4]{1,0:T(8,128)} %copy.79) | copy-start | bytes 36868
  231.1 264.2 %collective-permute-start.4 = (bf16[6144,4,128]{0,2,1:T(8,128)(2,1)}, bf16[6144,4,128]{0,2,1:T(8,128)(2,1)}, u32[]{:S(2)}, u32[]{:S(2)}) collective-permute-start(bf16[6144,4,128]{0,2,1:T(8,128)(2,1)} %maximum_select_fusion.2), channel_id=1, source_target_pairs={{0,16},{4,20},{8,24},{12,28},{16,0},{20,4},{24,8},{28,12},{32,48},... | collective-permute-start | bytes 18874376 | tf_op jit(solution)/shard_map/ppermute | solution.py:18
  259.4 8.6 %copy-start.26 = (pred[4,4]{0,1:T(4,128)(4,1)S(1)}, pred[4,4]{0,1:T(4,128)(4,1)}, u32[]{:S(2)}) copy-start(pred[4,4]{0,1:T(4,128)(4,1)} %copy-done.25) | copy-start | bytes 52
  268.0 42.8 %copy-start.9 = (pred[384,1536]{1,0:T(8,128)(4,1)S(1)}, pred[384,1536]{1,0:T(8,128)(4,1)}, u32[]{:S(2)}) copy-start(pred[384,1536]{1,0:T(8,128)(4,1)} %iota_compare_fusion.2) | copy-start | bytes 1769476
  268.0 42.8 %copy-start.11 = (bf16[384,4,128]{2,1,0:T(4,128)(2,1)S(1)}, bf16[384,4,128]{2,1,0:T(4,128)(2,1)}, u32[]{:S(2)}) copy-start(bf16[384,4,128]{2,1,0:T(4,128)(2,1)} %select_reduce_fusion.2) | copy-start | bytes 1179652
  527.3 38.2 %copy-start.13 = (bf16[192,4,128]{2,1,0:T(4,128)(2,1)S(1)}, bf16[192,4,128]{2,1,0:T(4,128)(2,1)}, u32[]{:S(2)}) copy-start(bf16[192,4,128]{2,1,0:T(4,128)(2,1)} %fusion.39) | copy-start | bytes 589828
  620.6 5.8 copy-start.7
  663.8 8.1 %copy-start.1 = (s32[3,16]{1,0:T(4,128)S(1)}, s32[3,16]{1,0:T(4,128)}, u32[]{:S(2)}) copy-start(s32[3,16]{1,0:T(4,128)} %param.10) | copy-start | bytes 580
  (12 other events, 29.0 us)
where the time goes:
time: 683 us; the launch traced here: 672 us
  other arithmetic  232 us (34%)
  local copies, waits for them, and re-layouts  210 us (31%)
  waiting for transfers between devices  137 us (20%)
  matrix products  58.1 us (9%)
  blocking collectives  24.1 us (4%)
  starting transfers between devices  9.23 us (1%)
    ppermute x6, waiting for transfers between devices, swapped(): return lax.ppermute(value, axis, pairs)  137 us
    reduce_sum x6, other arithmetic, pick_rows(): jnp.sum(jnp.where(hits[None, :, :, None], shaped, jnp.zeros((), source.dt...  133 us
    select_n x6, local copies, waits for them, and re-layouts, join_pair(): jnp.where(upper, jnp.concatenate([other_part, mine_part], 0), jnp.concate...  57.9 us
    select_n x6, other arithmetic, join_pair(): jnp.where(upper, jnp.concatenate([other_part, mine_part], 0), jnp.concate...  54.3 us
    dot_general x6, matrix products, one_block(): jnp.einsum('hqk,khd->qhd', weights.astype(jnp.bfloat16), value_rows, pref...  29.6 us
    reduce_sum x6, other arithmetic, one_block(): row_sum = jnp.sum(weights, axis=2)  27.9 us
    broadcast_in_dim x6, local copies, waits for them, and re-layouts, pick_rows(): jnp.where(hits[None, :, :, None], shaped, jnp.zeros((), source.dtype))  27.7 us
    all_to_all x1, blocking collectives, body(): lax.all_to_all(attended, 'head', split_axis=0, concat_axis=1, tiled=True)  24.1 us
  transfers between devices with their start and end apart: 6, of which 3 were waited for; matrix products, arithmetic and copies ran while one was open for 51% of the time, Pallas kernels for 0%

commit v1 on v0

v1 whole, which is shorter than its diff:
```python
import math

import jax
import jax.numpy as jnp
import numpy as np
from jax import lax
from jax.experimental import pallas as pl
from jax.experimental.pallas import tpu as pltpu
from jax.sharding import PartitionSpec as P

DH = 128
LEVELS = 4
CLASSES = 8
HEADS_HERE = 4
TOK = 1536
QUARTER = 384
RUN = QUARTER // CLASSES
SUB = 128
NEG = -1e30
SCALE = math.log2(math.e) / math.sqrt(DH)
MESH = pl.DeviceIdType.MESH
F32 = jnp.float32
BF16 = jnp.bfloat16

QC, KC, VC = 0, TOK, 2 * TOK
N1, N2, N3 = TOK // 2, TOK // 4, TOK // 8
Q1 = 3 * TOK
Q2 = Q1 + N1
Q3 = Q2 + N2
K1 = Q3 + N3
V1 = K1 + N1
K2 = V1 + N1
V2 = K2 + N2
K3 = V2 + N2
V3 = K3 + N3
ROWS = V3 + N3

R0, R1, R2, R3 = 0, TOK, TOK + N1, TOK + N1 + N2
RES = TOK + N1 + N2 + N3


def class_order(tokens):
    return np.arange(tokens).reshape(tokens // CLASSES, CLASSES).T.reshape(-1)


def pick_kernel(off_ref, perm_ref, q_ref, k_ref, v_ref, out_ref):
    head = lax.axis_index("head") * HEADS_HERE + pl.program_id(0)
    perm = perm_ref[...]
    run_sub = SUB // CLASSES
    for source, base in ((q_ref, QC), (k_ref, KC), (v_ref, VC)):
        for sub in range(TOK // SUB):
            moved = jnp.dot(
                perm, source[sub * SUB : (sub + 1) * SUB, :], preferred_element_type=F32
            ).astype(BF16)
            quarter, part = divmod(sub, QUARTER // SUB)
            for c in range(CLASSES):
                row = base + quarter * QUARTER + c * RUN + part * run_sub
                out_ref[0, row : row + run_sub, :] = moved[c * run_sub : (c + 1) * run_sub, :]
    for base, targets in ((QC, (Q1, Q2, Q3)), (KC, (K1, K2, K3)), (VC, (V1, V2, V3))):
        for level in range(1, LEVELS):
            dilation = 2**level
            runs = CLASSES // dilation
            shift = off_ref[level - 1, head]
            for quarter in range(TOK // QUARTER):
                for b in range(runs):
                    row = base + quarter * QUARTER + (dilation * b + shift) * RUN
                    row = pl.multiple_of(row, 16)
                    to = targets[level - 1] + (quarter * runs + b) * RUN
                    out_ref[0, to : to + RUN, :] = out_ref[0, pl.ds(row, RUN), :]


def scores_of(q, k):
    return lax.dot_general(q, k, (((1,), (1,)), ((), ())), preferred_element_type=F32)


def softmax_parts(parts):
    top = None
    for s, _, valid in parts:
        high = jnp.max(s, axis=1, keepdims=True)
        if valid is not None:
            high = jnp.where(valid, high, NEG)
        top = high if top is None else jnp.maximum(top, high)
    weights, values = [], []
    for s, v, valid in parts:
        if valid is None:
            base, one = top, jnp.ones(v.shape, BF16)
        else:
            base = jnp.where(valid, top, 0.0)
            one = jnp.full(v.shape, jnp.where(valid, 1.0, 0.0), F32).astype(BF16)
        weights.append(jnp.exp2((s - base) * SCALE).astype(BF16))
        values.append(jnp.concatenate([v, one], axis=1))
    out = jnp.dot(
        jnp.concatenate(weights, axis=1), jnp.concatenate(values, axis=0), preferred_element_type=F32
    )
    return top, out


def main_kernel(
    off_ref, qkv_hbm, w_hbm, unperm_ref, pq0, pq1, pq2, pk0, pk1, pk2, out_ref,
    qkv, kv1, kv2, kv3, w_vm, abuf, att, ap, res_m, res_l, res_a,
    load_sem, w_sem, r1, r2, r3, ra, s1, s2p, s2y, s2r, s3p, s3y, s3r, sa,
):
    ctx = lax.axis_index("ctx")
    x = lax.axis_index("head")
    core = ctx % 2
    y = (ctx // 2) % 4
    p4 = ctx % 4
    p8 = ctx % 8
    partner = ctx + 1 - 2 * core

    def at_y(step):
        return ctx + 2 * ((y + step) % 4 - y)

    def load(h):
        return pltpu.make_async_copy(qkv_hbm.at[h], qkv.at[h], load_sem.at[h])

    w_copy = pltpu.make_async_copy(w_hbm, w_vm, w_sem)
    for h in range(HEADS_HERE):
        load(h).start()
    w_copy.start()

    barrier = pltpu.get_barrier_semaphore()
    pl.semaphore_signal(barrier, inc=1, device_id={"ctx": partner, "head": x}, device_id_type=MESH)
    for step in range(1, 4):
        pl.semaphore_signal(barrier, inc=1, device_id={"ctx": at_y(step), "head": x}, device_id_type=MESH)
        pl.semaphore_signal(barrier, inc=1, device_id={"ctx": ctx, "head": (x + step) % 4}, device_id_type=MESH)
    pl.semaphore_wait(barrier, 7)

    def remote(source, target, send, recv, to_ctx, to_head):
        return pltpu.make_async_remote_copy(
            src_ref=source, dst_ref=target, send_sem=send, recv_sem=recv,
            device_id={"ctx": to_ctx, "head": to_head}, device_id_type=MESH,
        )

    def send1(h):
        return remote(qkv_hbm.at[h, pl.ds(K1, 2 * N1)], kv1.at[h], s1.at[h], r1.at[h], partner, x)

    def send2_partner(h):
        return remote(qkv_hbm.at[h, pl.ds(K2, 2 * N2)], kv2.at[0, h], s2p.at[h], r2.at[h, 1], partner, x)

    def send2_y(h):
        return remote(qkv_hbm.at[h, pl.ds(K2, 2 * N2)], kv2.at[1, h], s2y.at[h], r2.at[h, 2], at_y(1), x)

    def relay2(h):
        slot = 3 - 2 * core
        return remote(kv2.at[1, h], kv2.at[slot - 1, h], s2r.at[h], r2.at[h, slot], partner, x)

    def send3_partner(h):
        return remote(qkv_hbm.at[h, pl.ds(K3, 2 * N3)], kv3.at[0, h], s3p.at[h], r3.at[h, 1], partner, x)

    def send3_y(h, step):
        return remote(
            qkv_hbm.at[h, pl.ds(K3, 2 * N3)], kv3.at[2 * step - 1, h], s3y.at[h, step],
            r3.at[h, 2 * step], at_y(step), x,
        )

    def relay3(h, step):
        slot = 2 * step + 1 - 2 * core
        return remote(
            kv3.at[2 * step - 1, h], kv3.at[slot - 1, h], s3r.at[h, step], r3.at[h, slot], partner, x
        )

    def send_att(h, step):
        to = (x + step) % 4
        return remote(att.at[h, to], abuf.at[x * HEADS_HERE + h], sa.at[h, step], ra.at[h, step], ctx, to)

    def start_sends(h, carry):
        for step in (3, 2, 1):
            @pl.when(y + step <= 3)
            def _():
                send3_y(h, step).start()
        @pl.when(y % 2 == 0)
        def _():
            send2_y(h).start()
        @pl.when(core == 0)
        def _():
            send1(h).start()
            send2_partner(h).start()
            send3_partner(h).start()
        return carry

    lax.fori_loop(0, HEADS_HERE, start_sends, 0)

    @pl.when(core == 0)
    def _():
        kv1[...] = jnp.zeros(kv1.shape, BF16)
    for slot in range(1, 4):
        @pl.when(slot > p4)
        def _():
            kv2[slot - 1] = jnp.zeros(kv2.shape[1:], BF16)
    for slot in range(1, 8):
        @pl.when(slot > p8)
        def _():
            kv3[slot - 1] = jnp.zeros(kv3.shape[1:], BF16)

    def own(h, row, count):
        return qkv[h, row : row + count, :]

    def keep(row, count, top, out):
        res_m[row : row + count, :] = jnp.broadcast_to(top, (count, DH))
        res_a[row : row + count, :] = out[:, :DH]
        res_l[row : row + count, :] = out[:, DH:]

    def masked(s, pq, pk):
        seen = jnp.concatenate([pq[...]] * (QUARTER // DH), axis=1) >= pk[...]
        return jnp.where(seen, s, NEG)

    def one_head(h, carry):
        pltpu.make_async_copy(qkv_hbm.at[h], qkv.at[h], load_sem.at[h]).wait()
        for i in range(TOK // QUARTER):
            q = own(h, QC + i * QUARTER, QUARTER)
            parts = []
            s = scores_of(q, own(h, KC + i * QUARTER, QUARTER))
            parts.append((masked(s, pq0, pk0), own(h, VC + i * QUARTER, QUARTER), None))
            if i:
                parts.append((scores_of(q, own(h, KC, i * QUARTER)), own(h, VC, i * QUARTER), None))
            top, out = softmax_parts(parts)
            keep(R0 + i * QUARTER, QUARTER, top, out)
        @pl.when(y % 2 == 1)
        def _():
            send2_y(h).wait_recv()
            relay2(h).start()
        for step in (1, 2, 3):
            @pl.when(y >= step)
            def _():
                send3_y(h, step).wait_recv()
                relay3(h, step).start()
        @pl.when(core == 1)
        def _():
            send1(h).wait_recv()
        for i in range(N1 // QUARTER):
            q = own(h, Q1 + i * QUARTER, QUARTER)
            parts = []
            s = scores_of(q, own(h, K1 + i * QUARTER, QUARTER))
            parts.append((masked(s, pq1, pk1), own(h, V1 + i * QUARTER, QUARTER), None))
            if i:
                parts.append((scores_of(q, own(h, K1, i * QUARTER)), own(h, V1, i * QUARTER), None))
            parts.append((scores_of(q, kv1[h, :N1]), kv1[h, N1:], core == 1))
            top, out = softmax_parts(parts)
            keep(R1 + i * QUARTER, QUARTER, top, out)
        for slot in (1, 3):
            @pl.when(slot <= p4)
            def _():
                remote(kv2.at[0, h], kv2.at[slot - 1, h], s2r.at[h], r2.at[h, slot], partner, x).wait_recv()
        q = own(h, Q2, N2)
        parts = [(masked(scores_of(q, own(h, K2, N2)), pq2, pk2), own(h, V2, N2), None)]
        for slot in range(1, 4):
            parts.append((scores_of(q, kv2[slot - 1, h, :N2]), kv2[slot - 1, h, N2:], slot <= p4))
        top, out = softmax_parts(parts)
        keep(R2, N2, top, out)
        for slot in (1, 3, 5, 7):
            @pl.when(slot <= p8)
            def _():
                remote(kv3.at[0, h], kv3.at[slot - 1, h], s3p.at[h], r3.at[h, slot], partner, x).wait_recv()
        q = own(h, Q3, N3)
        keys = jnp.concatenate([own(h, K3, N3)] + [kv3[d, h, :N3] for d in range(7)], axis=0)
        vals = jnp.concatenate([own(h, V3, N3)] + [kv3[d, h, N3:] for d in range(7)], axis=0)
        column = lax.broadcasted_iota(jnp.int32, (1, TOK), 1)
        least = jnp.where(column < N3, column, jnp.where(column < N3 * (p8 + 1), -1, TOK))
        row = lax.broadcasted_iota(jnp.int32, (N3, TOK), 0)
        s = jnp.where(row >= least, scores_of(q, keys), NEG)
        top, out = softmax_parts([(s, vals, None)])
        keep(R3, N3, top, out)
        head = x * HEADS_HERE + h
        shifts = [off_ref[level - 1, head] for level in range(1, LEVELS)]
        for i in range(TOK // QUARTER):
            for c in range(CLASSES):
                rows = [R0 + i * QUARTER + c * RUN]
                picked = [None]
                for level, start in ((1, R1), (2, R2), (3, R3)):
                    dilation = 2**level
                    runs = CLASSES // dilation
                    rows.append(start + (i * runs + c // dilation) * RUN)
                    picked.append(shifts[level - 1] == c % dilation)
                tops = []
                for level in range(LEVELS):
                    m = res_m[rows[level] : rows[level] + RUN, :]
                    tops.append(m if level == 0 else jnp.where(picked[level], m, NEG))
                high = jnp.maximum(jnp.maximum(tops[0], tops[1]), jnp.maximum(tops[2], tops[3]))
                num = den = None
                for level in range(LEVELS):
                    f = jnp.exp2((tops[level] - high) * SCALE)
                    a = f * res_a[rows[level] : rows[level] + RUN, :]
                    l = f * res_l[rows[level] : rows[level] + RUN, :]
                    num = a if num is None else num + a
                    den = l if den is None else den + l
                att[h, i, c * RUN : (c + 1) * RUN, :] = (num / den).astype(BF16)
        for step in (2, 1, 3):
            send_att(h, step).start()
        abuf[x * HEADS_HERE + h] = att[h, x]
        return carry

    lax.fori_loop(0, HEADS_HERE, one_head, 0)

    w_copy.wait()

    def wait_att(h, carry):
        for step in range(1, 4):
            source = (x + 4 - step) % 4
            remote(
                att.at[h, 0], abuf.at[source * HEADS_HERE + h], sa.at[h, step], ra.at[h, step], ctx, (x + step) % 4
            ).wait_recv()
        return carry

    lax.fori_loop(0, HEADS_HERE, wait_att, 0)
    unperm = unperm_ref[...]
    for g in range(4):
        block = jnp.concatenate([abuf[4 * g + i] for i in range(4)], axis=1)
        ap[:, g * 512 : (g + 1) * 512] = jnp.dot(unperm, block, preferred_element_type=F32).astype(BF16)

    def project(n, carry):
        at = pl.multiple_of(n * 256, 256)
        out_ref[:, pl.ds(at, 256)] = jnp.dot(
            ap[...], w_vm[:, pl.ds(at, 256)], preferred_element_type=F32
        ).astype(BF16)
        return carry

    lax.fori_loop(0, 8, project, 0)

    def wait_sends(h, carry):
        for step in (3, 2, 1):
            @pl.when(y + step <= 3)
            def _():
                send3_y(h, step).wait_send()
            @pl.when(y >= step)
            def _():
                relay3(h, step).wait_send()
            send_att(h, step).wait_send()
        @pl.when(y % 2 == 0)
        def _():
            send2_y(h).wait_send()
        @pl.when(y % 2 == 1)
        def _():
            relay2(h).wait_send()
        @pl.when(core == 0)
        def _():
            send1(h).wait_send()
            send2_partner(h).wait_send()
            send3_partner(h).wait_send()
        return carry

    lax.fori_loop(0, HEADS_HERE, wait_sends, 0)


def positions(level):
    row = np.arange(QUARTER)
    if level == 0:
        c, j = row // RUN, row % RUN
        return CLASSES * j + c
    runs = CLASSES // 2**level
    block, b, j = row // (runs * RUN), row // RUN % runs, row % RUN
    return block * runs * RUN + runs * j + b


def body(queries, keys, values, offsets, out_weight):
    order = class_order(SUB)
    perm = jnp.asarray(np.eye(SUB)[order], BF16)
    packed = pl.pallas_call(
        pick_kernel,
        grid=(HEADS_HERE,),
        in_specs=[
            pl.BlockSpec(memory_space=pltpu.SMEM),
            pl.BlockSpec((SUB, SUB), lambda h: (0, 0)),
            pl.BlockSpec((TOK, DH), lambda h: (0, h)),
            pl.BlockSpec((TOK, DH), lambda h: (0, h)),
            pl.BlockSpec((TOK, DH), lambda h: (0, h)),
        ],
        out_specs=pl.BlockSpec((1, ROWS, DH), lambda h: (h, 0, 0)),
        out_shape=jax.ShapeDtypeStruct((HEADS_HERE, ROWS, DH), BF16),
        compiler_params=pltpu.CompilerParams(vmem_limit_bytes=40 * 2**20),
        name="pick",
    )(offsets, perm, queries, keys, values)

    unperm = jnp.asarray(np.eye(QUARTER)[class_order(QUARTER)].T, BF16)
    place = [positions(level) for level in range(3)]
    pq = [jnp.asarray(np.repeat(p[:, None], DH, 1), jnp.int32) for p in place]
    pk = [jnp.asarray(p[None, :], jnp.int32) for p in place]
    vm = pl.BlockSpec(memory_space=pltpu.VMEM)
    hbm = pl.BlockSpec(memory_space=pl.ANY)
    dma = pltpu.SemaphoreType.DMA
    return pl.pallas_call(
        main_kernel,
        in_specs=[pl.BlockSpec(memory_space=pltpu.SMEM), hbm, hbm] + [vm] * 7,
        out_specs=vm,
        out_shape=jax.ShapeDtypeStruct((QUARTER, 2048), BF16),
        scratch_shapes=[
            pltpu.VMEM((HEADS_HERE, ROWS, DH), BF16),
            pltpu.VMEM((HEADS_HERE, 2 * N1, DH), BF16),
            pltpu.VMEM((3, HEADS_HERE, 2 * N2, DH), BF16),
            pltpu.VMEM((7, HEADS_HERE, 2 * N3, DH), BF16),
            pltpu.VMEM((2048, 2048), BF16),
            pltpu.VMEM((16, QUARTER, DH), BF16),
            pltpu.VMEM((HEADS_HERE, 4, QUARTER, DH), BF16),
            pltpu.VMEM((QUARTER, 2048), BF16),
            pltpu.VMEM((RES, DH), F32),
            pltpu.VMEM((RES, DH), F32),
            pltpu.VMEM((RES, DH), F32),
            dma((4,)), dma,
            dma((4,)), dma((4, 4)), dma((4, 8)), dma((4, 4)),
            dma((4,)), dma((4,)), dma((4,)), dma((4,)),
            dma((4,)), dma((4, 4)), dma((4, 4)), dma((4, 4)),
        ],
        compiler_params=pltpu.CompilerParams(
            collective_id=0, has_side_effects=True, vmem_limit_bytes=62 * 2**20
        ),
        name="attend",
    )(offsets, packed, out_weight, unperm, *pq, *pk)


def solution(mesh):
    placed = (P("ctx", "head"), P("ctx", "head"), P("ctx", "head"), P(), P())
    return jax.shard_map(
        body, mesh=mesh, in_specs=placed, out_specs=P(("ctx", "head"), None), check_vma=False
    )
```

time: 683 us -> 77.9 us (0.11)
  the two profiles are of different devices: /device:TPU:0 before, /device:TPU:56 now
where the time goes in v1:
time: 77.9 us; the launch traced here: 77.5 us
  Pallas kernels  65.7 us (84%)
  local copies, waits for them, and re-layouts  11.8 us (15%)
    pallas_call x1, Pallas kernels, body(): pl.pallas_call(main_kernel, in_specs=[pl.BlockSpec(memory_space=pltpu.SME...  61.6 us
    unnamed x13, local copies, waits for them, and re-layouts  11.8 us
    pallas_call x1, Pallas kernels, body(): pl.pallas_call(pick_kernel, grid=(HEADS_HERE,), in_specs=[pl.BlockSpec(me...  4.14 us

profile of v1, /device:TPU:56, one launch (start us, length us, event | category | flops | bytes accessed | tf_op | source)
XLA Modules:
  0.0 77.5 jit_solution(17708569666315818048)
XLA Ops:
  0.0 0.0 copy-start.1
  0.0 1.4 %copy-done.1 = bf16[1536,512]{1,0:T(8,128)(2,1)S(1)} copy-done((bf16[1536,512]{1,0:T(8,128)(2,1)S(1)}, bf16[1536,512]{1,0:T(8,128)(2,1)}, u32[]{:S(2)}) %copy-start.1) | copy-done | bytes 1572888
  1.4 0.0 copy-start.2
  1.4 1.4 %copy-done.2 = bf16[1536,512]{1,0:T(8,128)(2,1)S(1)} copy-done((bf16[1536,512]{1,0:T(8,128)(2,1)S(1)}, bf16[1536,512]{1,0:T(8,128)(2,1)}, u32[]{:S(2)}) %copy-start.2) | copy-done | bytes 1572888
  2.8 0.0 copy-start.3
  2.8 1.4 %copy-done.3 = bf16[1536,512]{1,0:T(8,128)(2,1)S(1)} copy-done((bf16[1536,512]{1,0:T(8,128)(2,1)S(1)}, bf16[1536,512]{1,0:T(8,128)(2,1)}, u32[]{:S(2)}) %copy-start.3) | copy-done | bytes 1572888
  4.2 0.0 copy-start.4
  4.2 0.8 copy-done.4
  5.0 0.0 copy-start.5
  5.0 0.7 copy-done.5
  5.7 4.1 %pick.1.qkv_hbm = bf16[4,8640,128]{2,1,0:T(8,128)(2,1)S(1)} custom-call(s32[3,16]{1,0:T(4,128)S(1)} %copy-done.5, bf16[128,128]{1,0:T(8,128)(2,1)S(1)} %copy-done.4, bf16[1536,512]{1,0:T(8,128)(2,1)S(1)} %copy-done.1, bf16[1536,512]{1,0:T(8,128)(2,1)S(1)} %copy-done.2, bf16[1536,512]{1,0:T(8,128)(2,1)S(1)} %copy-done.3), custom_call_target="tpu_custom_call" | custom-call | tf_op jit(solution)/shard_map/pick/pallas_call | solution.py:358
  9.8 0.0 copy-start
  9.8 3.4 %copy-done = bf16[4,8640,128]{2,1,0:T(8,128)(2,1)} copy-done((bf16[4,8640,128]{2,1,0:T(8,128)(2,1)}, bf16[4,8640,128]{2,1,0:T(8,128)(2,1)S(1)}, u32[]{:S(2)}) %copy-start) | copy-done | bytes 8847384
  13.2 61.6 %attend.1 = bf16[384,2048]{1,0:T(8,128)(2,1)} custom-call(s32[3,16]{1,0:T(4,128)} %off_ref.3, bf16[4,8640,128]{2,1,0:T(8,128)(2,1)} %copy-done, bf16[2048,2048]{1,0:T(8,128)(2,1)} %w_hbm.1, bf16[384,384]{1,0:T(8,128)(2,1)} %constant.17.clone.unperm_ref, s32[384,128]{1,0:T(8,128)} %constant.18.clone.pq0, s32[384,128]{1,0:T(8,128)} %constant.19.clone.pq1, ...), custom_call_target="tpu_custom_call" | custom-call | tf_op jit(solution)/shard_map/attend/pallas_call | solution.py:381
  74.8 2.7 %copy.15 = bf16[384,2048]{1,0:T(8,128)(2,1)} copy(bf16[384,2048]{1,0:T(8,128)(2,1)} %attend.1) | data formatting | bytes 3145728
Async XLA Ops:
  0.0 1.4 %copy-start.1 = (bf16[1536,512]{1,0:T(8,128)(2,1)S(1)}, bf16[1536,512]{1,0:T(8,128)(2,1)}, u32[]{:S(2)}) copy-start(bf16[1536,512]{1,0:T(8,128)(2,1)} %q_ref.1) | copy-start | bytes 4718596
  1.4 1.4 %copy-start.2 = (bf16[1536,512]{1,0:T(8,128)(2,1)S(1)}, bf16[1536,512]{1,0:T(8,128)(2,1)}, u32[]{:S(2)}) copy-start(bf16[1536,512]{1,0:T(8,128)(2,1)} %k_ref.1) | copy-start | bytes 4718596
  2.8 1.4 %copy-start.3 = (bf16[1536,512]{1,0:T(8,128)(2,1)S(1)}, bf16[1536,512]{1,0:T(8,128)(2,1)}, u32[]{:S(2)}) copy-start(bf16[1536,512]{1,0:T(8,128)(2,1)} %v_ref.1) | copy-start | bytes 4718596
  4.2 0.8 copy-start.4
  5.0 0.7 copy-start.5
  9.8 3.4 %copy-start = (bf16[4,8640,128]{2,1,0:T(8,128)(2,1)}, bf16[4,8640,128]{2,1,0:T(8,128)(2,1)S(1)}, u32[]{:S(2)}) copy-start(bf16[4,8640,128]{2,1,0:T(8,128)(2,1)S(1)} %pick.1.qkv_hbm) | copy-start | bytes 26542084

commit v2 on v1

v2 whole, which is shorter than its diff:
```python
import math

import jax
import jax.numpy as jnp
import numpy as np
from jax import lax
from jax.experimental import pallas as pl
from jax.experimental.pallas import tpu as pltpu
from jax.sharding import PartitionSpec as P

DH = 128
LEVELS = 4
CLASSES = 8
HEADS_HERE = 4
TOK = 1536
QUARTER = 384
RUN = QUARTER // CLASSES
SUB = 128
NEG = -1e30
SCALE = math.log2(math.e) / math.sqrt(DH)
MESH = pl.DeviceIdType.MESH
F32 = jnp.float32
BF16 = jnp.bfloat16

QC, KC, VC = 0, TOK, 2 * TOK
N1, N2, N3 = TOK // 2, TOK // 4, TOK // 8
Q1 = 3 * TOK
Q2 = Q1 + N1
Q3 = Q2 + N2
K1 = Q3 + N3
V1 = K1 + N1
K2 = V1 + N1
V2 = K2 + N2
K3 = V2 + N2
V3 = K3 + N3
ROWS = V3 + N3

R2, R3 = 0, N2
RES = N2 + N3


def class_order(tokens):
    return np.arange(tokens).reshape(tokens // CLASSES, CLASSES).T.reshape(-1)


def pick_kernel(off_ref, perm_ref, q_ref, k_ref, v_ref, out_ref):
    head = lax.axis_index("head") * HEADS_HERE + pl.program_id(0)
    perm = perm_ref[...]
    run_sub = SUB // CLASSES
    for source, base in ((q_ref, QC), (k_ref, KC), (v_ref, VC)):
        for sub in range(TOK // SUB):
            moved = jnp.dot(
                perm, source[sub * SUB : (sub + 1) * SUB, :], preferred_element_type=F32
            ).astype(BF16)
            quarter, part = divmod(sub, QUARTER // SUB)
            for c in range(CLASSES):
                row = base + quarter * QUARTER + c * RUN + part * run_sub
                out_ref[0, row : row + run_sub, :] = moved[c * run_sub : (c + 1) * run_sub, :]
    for base, targets in ((QC, (Q1, Q2, Q3)), (KC, (K1, K2, K3)), (VC, (V1, V2, V3))):
        for level in range(1, LEVELS):
            dilation = 2**level
            runs = CLASSES // dilation
            shift = off_ref[level - 1, head]
            for quarter in range(TOK // QUARTER):
                for b in range(runs):
                    row = base + quarter * QUARTER + (dilation * b + shift) * RUN
                    row = pl.multiple_of(row, 16)
                    to = targets[level - 1] + (quarter * runs + b) * RUN
                    out_ref[0, to : to + RUN, :] = out_ref[0, pl.ds(row, RUN), :]


def scores_of(q, k):
    return lax.dot_general(q, k, (((1,), (1,)), ((), ())), preferred_element_type=F32)


def softmax_parts(parts):
    top = None
    for s, _, valid in parts:
        high = jnp.max(s, axis=1, keepdims=True)
        if valid is not None:
            high = jnp.where(valid, high, NEG)
        top = high if top is None else jnp.maximum(top, high)
    weights, values = [], []
    for s, v, valid in parts:
        if valid is None:
            base = top
        else:
            base = jnp.where(valid, top, -NEG)
        weights.append(jnp.exp2((s - base) * SCALE).astype(BF16))
        values.append(jnp.concatenate([v, jnp.ones(v.shape, BF16)], axis=1))
    out = jnp.dot(
        jnp.concatenate(weights, axis=1), jnp.concatenate(values, axis=0), preferred_element_type=F32
    )
    return top, out


def pipelined(tiles):
    parts = tiles[0][0]()
    for at, (_, finish) in enumerate(tiles):
        ahead = tiles[at + 1][0]() if at + 1 < len(tiles) else None
        finish(*softmax_parts(parts))
        parts = ahead


def main_kernel(
    off_ref, qkv_hbm, w_hbm, unperm_ref, pq0, pq1, pq2, pk0, pk1, pk2, out_ref,
    qkv, kv1, kv2, kv3, passing, qfar, farout, farstat, gota, gots, w_vm, abuf, att, ap, total, res0, res1, res_m, res_l, res_a,
    load_sem, w_sem, r1, r2, rq, rfa, rfs, r3, rp, ra, s1, s2p, sq, sfa, sfs, s3p, s3y, s3r, s3f, sa,
):
    ctx = lax.axis_index("ctx")
    x = lax.axis_index("head")
    core = ctx % 2
    y = (ctx // 2) % 4
    p8 = ctx % 8
    partner = ctx + 1 - 2 * core

    def at_y(step):
        return ctx + 2 * ((y + step) % 4 - y)

    def load(h):
        return pltpu.make_async_copy(qkv_hbm.at[h], qkv.at[h], load_sem.at[h])

    w_copy = pltpu.make_async_copy(w_hbm, w_vm, w_sem)
    for h in range(HEADS_HERE):
        load(h).start()

    barrier = pltpu.get_barrier_semaphore()
    pl.semaphore_signal(barrier, inc=1, device_id={"ctx": partner, "head": x}, device_id_type=MESH)
    for step in range(1, 4):
        pl.semaphore_signal(barrier, inc=1, device_id={"ctx": at_y(step), "head": x}, device_id_type=MESH)
        pl.semaphore_signal(barrier, inc=1, device_id={"ctx": ctx, "head": (x + step) % 4}, device_id_type=MESH)
    pl.semaphore_wait(barrier, 7)

    def remote(source, target, send, recv, to_ctx, to_head):
        return pltpu.make_async_remote_copy(
            src_ref=source, dst_ref=target, send_sem=send, recv_sem=recv,
            device_id={"ctx": to_ctx, "head": to_head}, device_id_type=MESH,
        )

    def send1(h):
        return remote(qkv_hbm.at[h, pl.ds(K1, 2 * N1)], kv1.at[h], s1.at[h], r1.at[h], partner, x)

    def send2_partner(h):
        return remote(qkv_hbm.at[h, pl.ds(K2, 2 * N2)], kv2.at[h], s2p.at[h], r2.at[h], partner, x)

    def send_q(h):
        return remote(qkv_hbm.at[h, pl.ds(Q2, N2)], qfar.at[h], sq.at[h], rq.at[h], at_y(3), x)

    def send_far(h):
        return remote(farout.at[h], gota.at[h], sfa.at[h], rfa.at[h], at_y(1), x)

    def send_stat(h):
        return remote(farstat.at[h], gots.at[h], sfs.at[h], rfs.at[h], at_y(1), x)

    def send3_partner(h):
        return remote(qkv_hbm.at[h, pl.ds(K3, 2 * N3)], kv3.at[0, h], s3p.at[h], r3.at[h, 1], partner, x)

    def send3_y(h, step):
        return remote(
            qkv_hbm.at[h, pl.ds(K3, 2 * N3)], kv3.at[2 * step - 1, h], s3y.at[h, step],
            r3.at[h, 2 * step], at_y(step), x,
        )

    def send3_via(h):
        return remote(qkv_hbm.at[h, pl.ds(K3, 2 * N3)], passing.at[h], s3y.at[h, 2], rp.at[h], at_y(3), x)

    def forward3_up(h):
        return remote(passing.at[h], kv3.at[3, h], s3f.at[h], r3.at[h, 4], at_y(3), x)

    def forward3_down(h):
        return remote(kv3.at[5, h], kv3.at[3, h], s3f.at[h], r3.at[h, 4], at_y(3), x)

    def relay3(h, step):
        slot = 2 * step + 1 - 2 * core
        return remote(
            kv3.at[2 * step - 1, h], kv3.at[slot - 1, h], s3r.at[h, step], r3.at[h, slot], partner, x
        )

    def send_att(h, step):
        to = (x + step) % 4
        return remote(att.at[h, to], abuf.at[x * HEADS_HERE + h], sa.at[h, step], ra.at[h, step], ctx, to)

    def start_sends(h, carry):
        @pl.when(y % 2 == 1)
        def _():
            send_q(h).start()
        @pl.when(y == 0)
        def _():
            send3_y(h, 3).start()
        @pl.when(y == 1)
        def _():
            send3_via(h).start()
        @pl.when(y <= 2)
        def _():
            send3_y(h, 1).start()
        send2_partner(h).start()
        @pl.when(core == 0)
        def _():
            send1(h).start()
            send3_partner(h).start()
        return carry

    lax.fori_loop(0, HEADS_HERE, start_sends, 0)

    def clear():
        @pl.when(core == 0)
        def _():
            kv1[...] = jnp.zeros(kv1.shape, BF16)
        for slot in range(1, 8):
            @pl.when(slot > p8)
            def _():
                kv3[slot - 1] = jnp.zeros(kv3.shape[1:], BF16)

    def own(h, row, count):
        return qkv[h, row : row + count, :]

    def keep(row, count, top, out):
        res_m[row : row + count, :] = jnp.broadcast_to(top, (count, DH))
        res_a[row : row + count, :] = out[:, :DH]
        res_l[row : row + count, :] = out[:, DH:]

    def masked(s, pq, pk):
        seen = jnp.concatenate([pq[...]] * (QUARTER // DH), axis=1) >= pk[...]
        return jnp.where(seen, s, NEG)

    def level0(h):
        pltpu.make_async_copy(qkv_hbm.at[h], qkv.at[h], load_sem.at[h]).wait()
        def tile(i):
            def scores():
                q = own(h, QC + i * QUARTER, QUARTER)
                near = masked(scores_of(q, own(h, KC + i * QUARTER, QUARTER)), pq0, pk0)
                parts = [(near, own(h, VC + i * QUARTER, QUARTER), None)]
                if i:
                    parts.append((scores_of(q, own(h, KC, i * QUARTER)), own(h, VC, i * QUARTER), None))
                return parts

            def finish(top, out):
                rows = slice(i * QUARTER, (i + 1) * QUARTER)
                res0[h % 3, 0, rows, :] = jnp.broadcast_to(top, (QUARTER, DH))
                res0[h % 3, 1, rows, :] = out[:, :DH]
                res0[h % 3, 2, rows, :] = out[:, DH:]

            return scores, finish

        pipelined([tile(i) for i in (3, 2, 1, 0)])

    def pass_far(h):
        @pl.when(y == 0)
        def _():
            send3_via(h).wait_recv()
            forward3_up(h).start()
        @pl.when(y == 3)
        def _():
            send3_y(h, 3).wait_recv()
            forward3_down(h).start()
            relay3(h, 3).start()

    def pass_near(h):
        for step in (1, 2):
            @pl.when(y >= step)
            def _():
                send3_y(h, step).wait_recv()
                relay3(h, step).start()

    def level1(h):
        @pl.when(core == 1)
        def _():
            send1(h).wait_recv()
        def tile(i):
            def scores():
                q = own(h, Q1 + i * QUARTER, QUARTER)
                near = masked(scores_of(q, own(h, K1 + i * QUARTER, QUARTER)), pq1, pk1)
                parts = [(near, own(h, V1 + i * QUARTER, QUARTER), None)]
                if i:
                    parts.append((scores_of(q, own(h, K1, i * QUARTER)), own(h, V1, i * QUARTER), None))
                parts.append((scores_of(q, kv1[h, :N1]), kv1[h, N1:], core == 1))
                return parts

            def finish(top, out):
                rows = slice(i * QUARTER, (i + 1) * QUARTER)
                res1[h % 2, 0, rows, :] = jnp.broadcast_to(top, (QUARTER, DH))
                res1[h % 2, 1, rows, :] = out[:, :DH]
                res1[h % 2, 2, rows, :] = out[:, DH:]

            return scores, finish

        pipelined([tile(1), tile(0)])

    def far(h):
        send_q(h).wait_recv()
        q = qfar[h]
        top, out = softmax_parts([
            (scores_of(q, own(h, K2, N2)), own(h, V2, N2), None),
            (scores_of(q, kv2[h, :N2]), kv2[h, N2:], None),
        ])
        farout[h] = out[:, :DH].astype(BF16)
        lane = lax.broadcasted_iota(jnp.int32, (N2, DH), 1)
        both = jnp.where(lane < DH // 2, jnp.broadcast_to(top, (N2, DH)), out[:, DH:]).T
        farstat[h, :8, :] = both[:8, :]
        farstat[h, 8:, :] = both[DH // 2 : DH // 2 + 8, :]
        send_far(h).start()
        send_stat(h).start()

    def join_far(h):
        send_far(h).wait_recv()
        send_stat(h).wait_recv()
        m_far = jnp.broadcast_to(gots[h, 0:1, :], (DH, N2)).T
        l_far = jnp.broadcast_to(gots[h, 8:9, :], (DH, N2)).T
        rows = slice(R2, R2 + N2)
        m = res_m[rows, :]
        high = jnp.maximum(m, m_far)
        here = jnp.exp2((m - high) * SCALE)
        there = jnp.exp2((m_far - high) * SCALE)
        res_m[rows, :] = high
        res_l[rows, :] = here * res_l[rows, :] + there * l_far
        res_a[rows, :] = here * res_a[rows, :] + there * gota[h].astype(F32)

    def rest(h):
        for slot in (1, 3, 5, 7):
            @pl.when(slot <= p8)
            def _():
                remote(kv3.at[0, h], kv3.at[slot - 1, h], s3p.at[h], r3.at[h, slot], partner, x).wait_recv()
        def scores2():
            q = own(h, Q2, N2)
            parts = [(masked(scores_of(q, own(h, K2, N2)), pq2, pk2), own(h, V2, N2), None)]
            parts.append((scores_of(q, kv2[h, :N2]), kv2[h, N2:], core == 1))
            return parts

        def scores3():
            keys = jnp.concatenate([own(h, K3, N3)] + [kv3[d, h, :N3] for d in range(7)], axis=0)
            vals = jnp.concatenate([own(h, V3, N3)] + [kv3[d, h, N3:] for d in range(7)], axis=0)
            column = lax.broadcasted_iota(jnp.int32, (1, TOK), 1)
            least = jnp.where(column < N3, column, jnp.where(column < N3 * (p8 + 1), -1, TOK))
            row = lax.broadcasted_iota(jnp.int32, (N3, TOK), 0)
            return [(jnp.where(row >= least, scores_of(own(h, Q3, N3), keys), NEG), vals, None)]

        head = x * HEADS_HERE + h
        shifts = [off_ref[level - 1, head] for level in range(1, LEVELS)]

        def joined(terms):
            high = terms[0][0]
            for m, _, _ in terms[1:]:
                high = jnp.maximum(high, m)
            num = den = None
            for m, a, l in terms:
                f = jnp.exp2((m - high) * SCALE)
                num = f * a if num is None else num + f * a
                den = f * l if den is None else den + f * l
            return high, num, den

        def base_term(i, c):
            rows = slice(i * QUARTER + c * RUN, i * QUARTER + c * RUN + RUN)
            return [res0[h % 3, part, rows, :] for part in range(3)]

        def level_term(level, start, i, c):
            dilation = 2**level
            at = start + (i * (CLASSES // dilation) + c // dilation) * RUN
            rows = slice(at, at + RUN)
            if level == 1:
                m, a, l = (res1[h % 2, part, rows, :] for part in range(3))
            else:
                m, a, l = res_m[rows, :], res_a[rows, :], res_l[rows, :]
            return jnp.where(shifts[level - 1] == c % dilation, m, NEG), a, l

        parts2 = scores2()
        parts3 = scores3()
        keep(R2, N2, *softmax_parts(parts2))
        keep(R3, N3, *softmax_parts(parts3))
        @pl.when(y % 2 == 1)
        def _():
            join_far(h)
        for i in range(TOK // QUARTER):
            for c in range(CLASSES):
                terms = [base_term(i, c)]
                for level, start in ((1, 0), (2, R2), (3, R3)):
                    terms.append(level_term(level, start, i, c))
                _, num, den = joined(terms)
                att[h, i, c * RUN : (c + 1) * RUN, :] = (num / den).astype(BF16)
        for step in (2, 1, 3):
            send_att(h, step).start()
        abuf[x * HEADS_HERE + h] = att[h, x]

    def one_step(step, carry):
        h = step - 1
        @pl.when(step < HEADS_HERE)
        def _():
            level0(step)
        @pl.when(step == 2)
        def _():
            w_copy.start()
        @pl.when(step >= 2)
        def _():
            pass_near(h - 1)
        @pl.when((h >= 0) & (h < HEADS_HERE))
        def _():
            level1(h)
            pass_far(h)
            send2_partner(h).wait_recv()
            @pl.when(y % 2 == 0)
            def _():
                far(h)
        @pl.when(step == 0)
        def _():
            clear()
        @pl.when(step >= 2)
        def _():
            rest(h - 1)
        return carry

    lax.fori_loop(0, HEADS_HERE + 2, one_step, 0)

    w_copy.wait()

    def wait_att(h, carry):
        for step in range(1, 4):
            source = (x + 4 - step) % 4
            remote(
                att.at[h, 0], abuf.at[source * HEADS_HERE + h], sa.at[h, step], ra.at[h, step], ctx, (x + step) % 4
            ).wait_recv()
        return carry

    unperm = unperm_ref[...]
    lax.fori_loop(0, HEADS_HERE - 1, wait_att, 0)
    for g in range(4):
        block = jnp.concatenate([abuf[4 * g + i] for i in range(3)], axis=1)
        ap[:, g * 384 : (g + 1) * 384] = jnp.dot(unperm, block, preferred_element_type=F32).astype(BF16)

    def project_first(n, carry):
        at = pl.multiple_of(n * 256, 256)
        weight = jnp.concatenate([w_vm[g * 512 : g * 512 + 384, pl.ds(at, 256)] for g in range(4)], axis=0)
        total[:, pl.ds(at, 256)] = jnp.dot(ap[:, :1536], weight, preferred_element_type=F32)
        return carry

    lax.fori_loop(0, 8, project_first, 0)
    wait_att(HEADS_HERE - 1, 0)
    block = jnp.concatenate([abuf[4 * g + 3] for g in range(4)], axis=1)
    ap[:, 1536:] = jnp.dot(unperm, block, preferred_element_type=F32).astype(BF16)

    def project_last(n, carry):
        at = pl.multiple_of(n * 256, 256)
        weight = jnp.concatenate([w_vm[g * 512 + 384 : g * 512 + 512, pl.ds(at, 256)] for g in range(4)], axis=0)
        out_ref[:, pl.ds(at, 256)] = (
            total[:, pl.ds(at, 256)] + jnp.dot(ap[:, 1536:], weight, preferred_element_type=F32)
        ).astype(BF16)
        return carry

    lax.fori_loop(0, 8, project_last, 0)

    def wait_sends(h, carry):
        @pl.when(y == 0)
        def _():
            send3_y(h, 3).wait_send()
            forward3_up(h).wait_send()
        @pl.when(y == 1)
        def _():
            send3_via(h).wait_send()
        @pl.when(y == 3)
        def _():
            forward3_down(h).wait_send()
        @pl.when(y <= 2)
        def _():
            send3_y(h, 1).wait_send()
        for step in (1, 2, 3):
            @pl.when(y >= step)
            def _():
                relay3(h, step).wait_send()
            send_att(h, step).wait_send()
        @pl.when(y % 2 == 0)
        def _():
            send_far(h).wait_send()
            send_stat(h).wait_send()
        @pl.when(y % 2 == 1)
        def _():
            send_q(h).wait_send()
        send2_partner(h).wait_send()
        @pl.when(core == 0)
        def _():
            send1(h).wait_send()
            send3_partner(h).wait_send()
        return carry

    lax.fori_loop(0, HEADS_HERE, wait_sends, 0)


def positions(level):
    row = np.arange(QUARTER)
    if level == 0:
        c, j = row // RUN, row % RUN
        return CLASSES * j + c
    runs = CLASSES // 2**level
    block, b, j = row // (runs * RUN), row // RUN % runs, row % RUN
    return block * runs * RUN + runs * j + b


def body(queries, keys, values, offsets, out_weight):
    order = class_order(SUB)
    perm = jnp.asarray(np.eye(SUB)[order], BF16)
    packed = pl.pallas_call(
        pick_kernel,
        grid=(HEADS_HERE,),
        in_specs=[
            pl.BlockSpec(memory_space=pltpu.SMEM),
            pl.BlockSpec((SUB, SUB), lambda h: (0, 0)),
            pl.BlockSpec((TOK, DH), lambda h: (0, h)),
            pl.BlockSpec((TOK, DH), lambda h: (0, h)),
            pl.BlockSpec((TOK, DH), lambda h: (0, h)),
        ],
        out_specs=pl.BlockSpec((1, ROWS, DH), lambda h: (h, 0, 0)),
        out_shape=jax.ShapeDtypeStruct((HEADS_HERE, ROWS, DH), BF16),
        compiler_params=pltpu.CompilerParams(vmem_limit_bytes=63 * 2**20),
        name="pick",
    )(offsets, perm, queries, keys, values)

    unperm = jnp.asarray(np.eye(QUARTER)[class_order(QUARTER)].T, BF16)
    place = [positions(level) for level in range(3)]
    pq = [jnp.asarray(np.repeat(p[:, None], DH, 1), jnp.int32) for p in place]
    pk = [jnp.asarray(p[None, :], jnp.int32) for p in place]
    vm = pl.BlockSpec(memory_space=pltpu.VMEM)
    hbm = pl.BlockSpec(memory_space=pl.ANY)
    dma = pltpu.SemaphoreType.DMA
    return pl.pallas_call(
        main_kernel,
        in_specs=[pl.BlockSpec(memory_space=pltpu.SMEM), hbm, hbm] + [vm] * 7,
        out_specs=vm,
        out_shape=jax.ShapeDtypeStruct((QUARTER, 2048), BF16),
        scratch_shapes=[
            pltpu.VMEM((HEADS_HERE, ROWS, DH), BF16),
            pltpu.VMEM((HEADS_HERE, 2 * N1, DH), BF16),
            pltpu.VMEM((HEADS_HERE, 2 * N2, DH), BF16),
            pltpu.VMEM((7, HEADS_HERE, 2 * N3, DH), BF16),
            pltpu.VMEM((HEADS_HERE, 2 * N3, DH), BF16),
            pltpu.VMEM((HEADS_HERE, N2, DH), BF16),
            pltpu.VMEM((HEADS_HERE, N2, DH), BF16),
            pltpu.VMEM((HEADS_HERE, 16, N2), F32),
            pltpu.VMEM((HEADS_HERE, N2, DH), BF16),
            pltpu.VMEM((HEADS_HERE, 16, N2), F32),
            pltpu.VMEM((2048, 2048), BF16),
            pltpu.VMEM((16, QUARTER, DH), BF16),
            pltpu.VMEM((HEADS_HERE, 4, QUARTER, DH), BF16),
            pltpu.VMEM((QUARTER, 2048), BF16),
            pltpu.VMEM((QUARTER, 2048), F32),
            pltpu.VMEM((3, 3, TOK, DH), F32),
            pltpu.VMEM((2, 3, N1, DH), F32),
            pltpu.VMEM((RES, DH), F32),
            pltpu.VMEM((RES, DH), F32),
            pltpu.VMEM((RES, DH), F32),
            dma((4,)), dma,
            dma((4,)), dma((4,)), dma((4,)), dma((4,)), dma((4,)), dma((4, 8)), dma((4,)), dma((4, 4)),
            dma((4,)), dma((4,)), dma((4,)), dma((4,)), dma((4,)),
            dma((4,)), dma((4, 4)), dma((4, 4)), dma((4,)), dma((4, 4)),
        ],
        compiler_params=pltpu.CompilerParams(
            collective_id=0, has_side_effects=True, vmem_limit_bytes=62 * 2**20
        ),
        name="attend",
    )(offsets, packed, out_weight, unperm, *pq, *pk)


def solution(mesh):
    placed = (P("ctx", "head"), P("ctx", "head"), P("ctx", "head"), P(), P())
    return jax.shard_map(
        body, mesh=mesh, in_specs=placed, out_specs=P(("ctx", "head"), None), check_vma=False
    )
```

time: 77.9 us -> 59.4 us (0.76)
  the two profiles are of different devices: /device:TPU:56 before, /device:TPU:0 now
where the time goes in v2:
time: 59.4 us; the launch traced here: 58.9 us
  Pallas kernels  56.1 us (94%)
  local copies, waits for them, and re-layouts  2.73 us (5%)
    pallas_call x1, Pallas kernels, body(): pl.pallas_call(main_kernel, in_specs=[pl.BlockSpec(memory_space=pltpu.SME...  48.5 us
    pallas_call x1, Pallas kernels, body(): pl.pallas_call(pick_kernel, grid=(HEADS_HERE,), in_specs=[pl.BlockSpec(me...  7.6 us
    unnamed x1, local copies, waits for them, and re-layouts  2.73 us

profile of v2, /device:TPU:0, one launch (start us, length us, event | category | flops | bytes accessed | tf_op | source)
XLA Modules:
  0.0 58.9 jit_solution(4097920887063195531)
XLA Ops:
  0.0 7.6 %pick.1.qkv_hbm = bf16[4,8640,128]{2,1,0:T(8,128)(2,1)} custom-call(s32[3,16]{1,0:T(4,128)} %off_ref.3, bf16[128,128]{1,0:T(8,128)(2,1)} %constant.16.clone.perm_ref, bf16[1536,512]{1,0:T(8,128)(2,1)} %q_ref.1, bf16[1536,512]{1,0:T(8,128)(2,1)} %k_ref.1, bf16[1536,512]{1,0:T(8,128)(2,1)} %v_ref.1), custom_call_target="tpu_custom_call" | custom-call | tf_op jit(solution)/shard_map/pick/pallas_call | solution.py:498
  7.6 48.5 %attend.1 = bf16[384,2048]{1,0:T(8,128)(2,1)} custom-call(s32[3,16]{1,0:T(4,128)} %off_ref.3, bf16[4,8640,128]{2,1,0:T(8,128)(2,1)} %pick.1.qkv_hbm, bf16[2048,2048]{1,0:T(8,128)(2,1)} %w_hbm.1, bf16[384,384]{1,0:T(8,128)(2,1)} %constant.17.clone.unperm_ref, s32[384,128]{1,0:T(8,128)} %constant.18.clone.pq0, s32[384,128]{1,0:T(8,128)} %constant.19.clone.pq1, ...), custom_call_target="tpu_custom_call" | custom-call | tf_op jit(solution)/shard_map/attend/pallas_call | solution.py:521
  56.2 2.7 %copy.15 = bf16[384,2048]{1,0:T(8,128)(2,1)} copy(bf16[384,2048]{1,0:T(8,128)(2,1)} %attend.1) | data formatting | bytes 3145728

commit v3 on v2

--- a/solution.py
+++ b/solution.py
@@ -41,32 +41,6 @@
 
 def class_order(tokens):
     return np.arange(tokens).reshape(tokens // CLASSES, CLASSES).T.reshape(-1)
-
-
-def pick_kernel(off_ref, perm_ref, q_ref, k_ref, v_ref, out_ref):
-    head = lax.axis_index("head") * HEADS_HERE + pl.program_id(0)
-    perm = perm_ref[...]
-    run_sub = SUB // CLASSES
-    for source, base in ((q_ref, QC), (k_ref, KC), (v_ref, VC)):
-        for sub in range(TOK // SUB):
-            moved = jnp.dot(
-                perm, source[sub * SUB : (sub + 1) * SUB, :], preferred_element_type=F32
-            ).astype(BF16)
-            quarter, part = divmod(sub, QUARTER // SUB)
-            for c in range(CLASSES):
-                row = base + quarter * QUARTER + c * RUN + part * run_sub
-                out_ref[0, row : row + run_sub, :] = moved[c * run_sub : (c + 1) * run_sub, :]
-    for base, targets in ((QC, (Q1, Q2, Q3)), (KC, (K1, K2, K3)), (VC, (V1, V2, V3))):
-        for level in range(1, LEVELS):
-            dilation = 2**level
-            runs = CLASSES // dilation
-            shift = off_ref[level - 1, head]
-            for quarter in range(TOK // QUARTER):
-                for b in range(runs):
-                    row = base + quarter * QUARTER + (dilation * b + shift) * RUN
-                    row = pl.multiple_of(row, 16)
-                    to = targets[level - 1] + (quarter * runs + b) * RUN
-                    out_ref[0, to : to + RUN, :] = out_ref[0, pl.ds(row, RUN), :]
 
 
 def scores_of(q, k):
@@ -103,8 +77,8 @@
 
 
 def main_kernel(
-    off_ref, qkv_hbm, w_hbm, unperm_ref, pq0, pq1, pq2, pk0, pk1, pk2, out_ref,
-    qkv, kv1, kv2, kv3, passing, qfar, farout, farstat, gota, gots, w_vm, abuf, att, ap, total, res0, res1, res_m, res_l, res_a,
+    off_ref, q_hbm, k_hbm, v_hbm, w_hbm, perm_ref, unperm_ref, pq0, pq1, pq2, pk0, pk1, pk2, out_ref,
+    raw, qkv, kv1, kv2, kv3, passing, qfar, farout, farstat, gota, gots, w_vm, abuf, att, ap, total, res0, res1, res_m, res_l, res_a,
     load_sem, w_sem, r1, r2, rq, rfa, rfs, r3, rp, ra, s1, s2p, sq, sfa, sfs, s3p, s3y, s3r, s3f, sa,
 ):
     ctx = lax.axis_index("ctx")
@@ -117,12 +91,16 @@
     def at_y(step):
         return ctx + 2 * ((y + step) % 4 - y)
 
-    def load(h):
-        return pltpu.make_async_copy(qkv_hbm.at[h], qkv.at[h], load_sem.at[h])
+    def load(h, which):
+        source = (q_hbm, k_hbm, v_hbm)[which]
+        return pltpu.make_async_copy(
+            source.at[:, pl.ds(h * DH, DH)], raw.at[h, which], load_sem.at[h, which]
+        )
 
     w_copy = pltpu.make_async_copy(w_hbm, w_vm, w_sem)
     for h in range(HEADS_HERE):
-        load(h).start()
+        for which in range(3):
+            load(h, which).start()
 
     barrier = pltpu.get_barrier_semaphore()
     pl.semaphore_signal(barrier, inc=1, device_id={"ctx": partner, "head": x}, device_id_type=MESH)
@@ -138,13 +116,13 @@
         )
 
     def send1(h):
-        return remote(qkv_hbm.at[h, pl.ds(K1, 2 * N1)], kv1.at[h], s1.at[h], r1.at[h], partner, x)
+        return remote(qkv.at[h, pl.ds(K1, 2 * N1)], kv1.at[h], s1.at[h], r1.at[h], partner, x)
 
     def send2_partner(h):
-        return remote(qkv_hbm.at[h, pl.ds(K2, 2 * N2)], kv2.at[h], s2p.at[h], r2.at[h], partner, x)
+        return remote(qkv.at[h, pl.ds(K2, 2 * N2)], kv2.at[h], s2p.at[h], r2.at[h], partner, x)
 
     def send_q(h):
-        return remote(qkv_hbm.at[h, pl.ds(Q2, N2)], qfar.at[h], sq.at[h], rq.at[h], at_y(3), x)
+        return remote(qkv.at[h, pl.ds(Q2, N2)], qfar.at[h], sq.at[h], rq.at[h], at_y(3), x)
 
     def send_far(h):
         return remote(farout.at[h], gota.at[h], sfa.at[h], rfa.at[h], at_y(1), x)
@@ -153,16 +131,16 @@
         return remote(farstat.at[h], gots.at[h], sfs.at[h], rfs.at[h], at_y(1), x)
 
     def send3_partner(h):
-        return remote(qkv_hbm.at[h, pl.ds(K3, 2 * N3)], kv3.at[0, h], s3p.at[h], r3.at[h, 1], partner, x)
+        return remote(qkv.at[h, pl.ds(K3, 2 * N3)], kv3.at[0, h], s3p.at[h], r3.at[h, 1], partner, x)
 
     def send3_y(h, step):
         return remote(
-            qkv_hbm.at[h, pl.ds(K3, 2 * N3)], kv3.at[2 * step - 1, h], s3y.at[h, step],
+            qkv.at[h, pl.ds(K3, 2 * N3)], kv3.at[2 * step - 1, h], s3y.at[h, step],
             r3.at[h, 2 * step], at_y(step), x,
         )
 
     def send3_via(h):
-        return remote(qkv_hbm.at[h, pl.ds(K3, 2 * N3)], passing.at[h], s3y.at[h, 2], rp.at[h], at_y(3), x)
+        return remote(qkv.at[h, pl.ds(K3, 2 * N3)], passing.at[h], s3y.at[h, 2], rp.at[h], at_y(3), x)
 
     def forward3_up(h):
         return remote(passing.at[h], kv3.at[3, h], s3f.at[h], r3.at[h, 4], at_y(3), x)
@@ -200,14 +178,54 @@
             send3_partner(h).start()
         return carry
 
-    lax.fori_loop(0, HEADS_HERE, start_sends, 0)
+    def pick(h, carry):
+        head = x * HEADS_HERE + h
+        perm = perm_ref[...]
+        run_sub = SUB // CLASSES
+        for which in range(3):
+            pltpu.make_async_copy(q_hbm.at[:, pl.ds(0, DH)], raw.at[h, which], load_sem.at[h, which]).wait()
+        pieces = [(which, base, sub) for sub in range(TOK // SUB) for which, base in enumerate((QC, KC, VC))]
+        for first in range(0, len(pieces), 6):
+            group = pieces[first : first + 6]
+            block = jnp.concatenate(
+                [raw[h, which, sub * SUB : (sub + 1) * SUB, :] for which, _, sub in group], axis=1
+            )
+            moved = jnp.dot(perm, block, preferred_element_type=F32).astype(BF16)
+            for at, (_, base, sub) in enumerate(group):
+                quarter, part = divmod(sub, QUARTER // SUB)
+                for c in range(CLASSES):
+                    row = base + quarter * QUARTER + c * RUN + part * run_sub
+                    qkv[h, row : row + run_sub, :] = moved[
+                        c * run_sub : (c + 1) * run_sub, at * DH : (at + 1) * DH
+                    ]
+        for base, targets in ((QC, (Q1, Q2, Q3)), (KC, (K1, K2, K3)), (VC, (V1, V2, V3))):
+            for level in range(1, LEVELS):
+                dilation = 2**level
+                runs = CLASSES // dilation
+                shift = off_ref[level - 1, head]
+                for quarter in range(TOK // QUARTER):
+                    for b in range(runs):
+                        row = base + quarter * QUARTER + dilation * b * RUN
+                        to = targets[level - 1] + (quarter * runs + b) * RUN
+                        found = qkv[h, row : row + RUN, :]
+                        for c in range(1, dilation):
+                            other = qkv[h, row + c * RUN : row + c * RUN + RUN, :]
+                            found = jnp.where(shift == c, other, found)
+                        qkv[h, to : to + RUN, :] = found
+        @pl.when(h > 0)
+        def _():
+            start_sends(h - 1, 0)
+        return carry
+
+    lax.fori_loop(0, HEADS_HERE, pick, 0)
+    start_sends(HEADS_HERE - 1, 0)
 
     def clear():
         @pl.when(core == 0)
         def _():
             kv1[...] = jnp.zeros(kv1.shape, BF16)
         for slot in range(1, 8):
-            @pl.when(slot > p8)
+            @pl.when((slot > p8) & ((y > 0) | (slot == 1)))
             def _():
                 kv3[slot - 1] = jnp.zeros(kv3.shape[1:], BF16)
 
@@ -224,7 +242,6 @@
         return jnp.where(seen, s, NEG)
 
     def level0(h):
-        pltpu.make_async_copy(qkv_hbm.at[h], qkv.at[h], load_sem.at[h]).wait()
         def tile(i):
             def scores():
                 q = own(h, QC + i * QUARTER, QUARTER)
@@ -326,12 +343,13 @@
             parts.append((scores_of(q, kv2[h, :N2]), kv2[h, N2:], core == 1))
             return parts
 
-        def scores3():
-            keys = jnp.concatenate([own(h, K3, N3)] + [kv3[d, h, :N3] for d in range(7)], axis=0)
-            vals = jnp.concatenate([own(h, V3, N3)] + [kv3[d, h, N3:] for d in range(7)], axis=0)
-            column = lax.broadcasted_iota(jnp.int32, (1, TOK), 1)
+        def scores3(slots):
+            width = (slots + 1) * N3
+            keys = jnp.concatenate([own(h, K3, N3)] + [kv3[d, h, :N3] for d in range(slots)], axis=0)
+            vals = jnp.concatenate([own(h, V3, N3)] + [kv3[d, h, N3:] for d in range(slots)], axis=0)
+            column = lax.broadcasted_iota(jnp.int32, (1, width), 1)
             least = jnp.where(column < N3, column, jnp.where(column < N3 * (p8 + 1), -1, TOK))
-            row = lax.broadcasted_iota(jnp.int32, (N3, TOK), 0)
+            row = lax.broadcasted_iota(jnp.int32, (N3, width), 0)
             return [(jnp.where(row >= least, scores_of(own(h, Q3, N3), keys), NEG), vals, None)]
 
         head = x * HEADS_HERE + h
@@ -362,10 +380,18 @@
                 m, a, l = res_m[rows, :], res_a[rows, :], res_l[rows, :]
             return jnp.where(shifts[level - 1] == c % dilation, m, NEG), a, l
 
-        parts2 = scores2()
-        parts3 = scores3()
-        keep(R2, N2, *softmax_parts(parts2))
-        keep(R3, N3, *softmax_parts(parts3))
+        def levels23(slots):
+            parts2 = scores2()
+            parts3 = scores3(slots)
+            keep(R2, N2, *softmax_parts(parts2))
+            keep(R3, N3, *softmax_parts(parts3))
+
+        @pl.when(y == 0)
+        def _():
+            levels23(1)
+        @pl.when(y > 0)
+        def _():
+            levels23(7)
         @pl.when(y % 2 == 1)
         def _():
             join_far(h)
@@ -426,25 +452,25 @@
         ap[:, g * 384 : (g + 1) * 384] = jnp.dot(unperm, block, preferred_element_type=F32).astype(BF16)
 
     def project_first(n, carry):
-        at = pl.multiple_of(n * 256, 256)
-        weight = jnp.concatenate([w_vm[g * 512 : g * 512 + 384, pl.ds(at, 256)] for g in range(4)], axis=0)
-        total[:, pl.ds(at, 256)] = jnp.dot(ap[:, :1536], weight, preferred_element_type=F32)
-        return carry
-
-    lax.fori_loop(0, 8, project_first, 0)
+        at = pl.multiple_of(n * 512, 512)
+        weight = jnp.concatenate([w_vm[g * 512 : g * 512 + 384, pl.ds(at, 512)] for g in range(4)], axis=0)
+        total[:, pl.ds(at, 512)] = jnp.dot(ap[:, :1536], weight, preferred_element_type=F32)
+        return carry
+
+    lax.fori_loop(0, 4, project_first, 0)
     wait_att(HEADS_HERE - 1, 0)
     block = jnp.concatenate([abuf[4 * g + 3] for g in range(4)], axis=1)
     ap[:, 1536:] = jnp.dot(unperm, block, preferred_element_type=F32).astype(BF16)
 
     def project_last(n, carry):
-        at = pl.multiple_of(n * 256, 256)
-        weight = jnp.concatenate([w_vm[g * 512 + 384 : g * 512 + 512, pl.ds(at, 256)] for g in range(4)], axis=0)
-        out_ref[:, pl.ds(at, 256)] = (
-            total[:, pl.ds(at, 256)] + jnp.dot(ap[:, 1536:], weight, preferred_element_type=F32)
+        at = pl.multiple_of(n * 512, 512)
+        weight = jnp.concatenate([w_vm[g * 512 + 384 : g * 512 + 512, pl.ds(at, 512)] for g in range(4)], axis=0)
+        out_ref[:, pl.ds(at, 512)] = (
+            total[:, pl.ds(at, 512)] + jnp.dot(ap[:, 1536:], weight, preferred_element_type=F32)
         ).astype(BF16)
         return carry
 
-    lax.fori_loop(0, 8, project_last, 0)
+    lax.fori_loop(0, 4, project_last, 0)
 
     def wait_sends(h, carry):
         @pl.when(y == 0)
@@ -495,22 +521,6 @@
 def body(queries, keys, values, offsets, out_weight):
     order = class_order(SUB)
     perm = jnp.asarray(np.eye(SUB)[order], BF16)
-    packed = pl.pallas_call(
-        pick_kernel,
-        grid=(HEADS_HERE,),
-        in_specs=[
-            pl.BlockSpec(memory_space=pltpu.SMEM),
-            pl.BlockSpec((SUB, SUB), lambda h: (0, 0)),
-            pl.BlockSpec((TOK, DH), lambda h: (0, h)),
-            pl.BlockSpec((TOK, DH), lambda h: (0, h)),
-            pl.BlockSpec((TOK, DH), lambda h: (0, h)),
-        ],
-        out_specs=pl.BlockSpec((1, ROWS, DH), lambda h: (h, 0, 0)),
-        out_shape=jax.ShapeDtypeStruct((HEADS_HERE, ROWS, DH), BF16),
-        compiler_params=pltpu.CompilerParams(vmem_limit_bytes=63 * 2**20),
-        name="pick",
-    )(offsets, perm, queries, keys, values)
-
     unperm = jnp.asarray(np.eye(QUARTER)[class_order(QUARTER)].T, BF16)
     place = [positions(level) for level in range(3)]
     pq = [jnp.asarray(np.repeat(p[:, None], DH, 1), jnp.int32) for p in place]
@@ -520,10 +530,11 @@
     dma = pltpu.SemaphoreType.DMA
     return pl.pallas_call(
         main_kernel,
-        in_specs=[pl.BlockSpec(memory_space=pltpu.SMEM), hbm, hbm] + [vm] * 7,
+        in_specs=[pl.BlockSpec(memory_space=pltpu.SMEM)] + [hbm] * 4 + [vm] * 8,
         out_specs=vm,
         out_shape=jax.ShapeDtypeStruct((QUARTER, 2048), BF16),
         scratch_shapes=[
+            pltpu.VMEM((HEADS_HERE, 3, TOK, DH), BF16),
             pltpu.VMEM((HEADS_HERE, ROWS, DH), BF16),
             pltpu.VMEM((HEADS_HERE, 2 * N1, DH), BF16),
             pltpu.VMEM((HEADS_HERE, 2 * N2, DH), BF16),
@@ -544,7 +555,7 @@
             pltpu.VMEM((RES, DH), F32),
             pltpu.VMEM((RES, DH), F32),
             pltpu.VMEM((RES, DH), F32),
-            dma((4,)), dma,
+            dma((4, 3)), dma,
             dma((4,)), dma((4,)), dma((4,)), dma((4,)), dma((4,)), dma((4, 8)), dma((4,)), dma((4, 4)),
             dma((4,)), dma((4,)), dma((4,)), dma((4,)), dma((4,)),
             dma((4,)), dma((4, 4)), dma((4, 4)), dma((4,)), dma((4, 4)),
@@ -553,7 +564,7 @@
             collective_id=0, has_side_effects=True, vmem_limit_bytes=62 * 2**20
         ),
         name="attend",
-    )(offsets, packed, out_weight, unperm, *pq, *pk)
+    )(offsets, queries, keys, values, out_weight, perm, unperm, *pq, *pk)
 
 
 def solution(mesh):

time: 59.4 us -> 51.5 us (0.87)
  Pallas kernels: 56.1 us -> 48.2 us
    pallas_call x1 -> x0, Pallas kernels: 7.6 us -> none  [body(): pl.pallas_call(pick_kernel, grid=(HEADS_HERE,), in_specs=[pl.BlockSpec(me...]
where the time goes in v3:
time: 51.5 us; the launch traced here: 51 us
  Pallas kernels  48.2 us (94%)
  local copies, waits for them, and re-layouts  2.73 us (5%)
    pallas_call x1, Pallas kernels, body(): pl.pallas_call(main_kernel, in_specs=[pl.BlockSpec(memory_space=pltpu.SME...  48.2 us
    unnamed x1, local copies, waits for them, and re-layouts  2.73 us

profile of v3, /device:TPU:0, one launch (start us, length us, event | category | flops | bytes accessed | tf_op | source)
XLA Modules:
  0.0 51.0 jit_solution(1819398185373611736)
XLA Ops:
  0.0 48.2 %attend.1 = bf16[384,2048]{1,0:T(8,128)(2,1)} custom-call(s32[3,16]{1,0:T(4,128)} %off_ref.1, bf16[1536,512]{1,0:T(8,128)(2,1)} %q_hbm.1, bf16[1536,512]{1,0:T(8,128)(2,1)} %k_hbm.1, bf16[1536,512]{1,0:T(8,128)(2,1)} %v_hbm.1, bf16[2048,2048]{1,0:T(8,128)(2,1)} %w_hbm.1, bf16[128,128]{1,0:T(8,128)(2,1)} %constant.16.clone.perm_ref, ...), custom_call_target="tpu_custom_call" | custom-call | tf_op jit(solution)/shard_map/attend/pallas_call | solution.py:531
  48.2 2.7 %copy.15 = bf16[384,2048]{1,0:T(8,128)(2,1)} copy(bf16[384,2048]{1,0:T(8,128)(2,1)} %attend.1) | data formatting | bytes 3145728

commit v4 on v3

--- a/solution.py
+++ b/solution.py
@@ -447,9 +447,8 @@
 
     unperm = unperm_ref[...]
     lax.fori_loop(0, HEADS_HERE - 1, wait_att, 0)
-    for g in range(4):
-        block = jnp.concatenate([abuf[4 * g + i] for i in range(3)], axis=1)
-        ap[:, g * 384 : (g + 1) * 384] = jnp.dot(unperm, block, preferred_element_type=F32).astype(BF16)
+    block = jnp.concatenate([abuf[4 * g + i] for g in range(4) for i in range(3)], axis=1)
+    ap[:, :1536] = jnp.dot(unperm, block, preferred_element_type=F32).astype(BF16)
 
     def project_first(n, carry):
         at = pl.multiple_of(n * 512, 512)

time: 51.5 us -> 51.5 us (level)
  no operation moved by 1% of the time
where the time goes in v4:
time: 51.5 us; the launch traced here: 50.9 us
  Pallas kernels  48.2 us (94%)
  local copies, waits for them, and re-layouts  2.73 us (5%)
    pallas_call x1, Pallas kernels, body(): pl.pallas_call(main_kernel, in_specs=[pl.BlockSpec(memory_space=pltpu.SME...  48.2 us
    unnamed x1, local copies, waits for them, and re-layouts  2.73 us

profile of v4, /device:TPU:0, one launch (start us, length us, event | category | flops | bytes accessed | tf_op | source)
XLA Modules:
  0.0 50.9 jit_solution(2347155793088670383)
XLA Ops:
  0.0 48.2 %attend.1 = bf16[384,2048]{1,0:T(8,128)(2,1)} custom-call(s32[3,16]{1,0:T(4,128)} %off_ref.1, bf16[1536,512]{1,0:T(8,128)(2,1)} %q_hbm.1, bf16[1536,512]{1,0:T(8,128)(2,1)} %k_hbm.1, bf16[1536,512]{1,0:T(8,128)(2,1)} %v_hbm.1, bf16[2048,2048]{1,0:T(8,128)(2,1)} %w_hbm.1, bf16[128,128]{1,0:T(8,128)(2,1)} %constant.16.clone.perm_ref, ...), custom_call_target="tpu_custom_call" | custom-call | tf_op jit(solution)/shard_map/attend/pallas_call | solution.py:530
  48.2 2.7 %copy.15 = bf16[384,2048]{1,0:T(8,128)(2,1)} copy(bf16[384,2048]{1,0:T(8,128)(2,1)} %attend.1) | data formatting | bytes 3145728
